TPU v7x, 256 devices: a whole 4x4x8 slice. The times are simulated.
256 devices in a mesh: samp: 32 (over x, z), reg: 8 (over y, core).
Axes of the slice: x: 4, y: 4, z: 8, core: 2. Of those that a mesh axis runs over, the one named last changes fastest.
Arguments:
- library: bfloat16 [98304, 1024], P('samp'), as said below
- responses: bfloat16 [98304, 1024], P('samp', 'reg'), as said below
- coefficients: float32 [1024, 1024], P(None, 'reg'), as said below
Outputs:
- updated: float32 [1024, 1024], P(None, 'reg')
Inputs may be any that keep to these rules, and one draw needn't show every extreme that they name: library entries are finite; column and row scales differ. responses are finite. coefficients are finite.
All inputs are finite; a program needn't handle non-finite values.
Results may differ from a plain program's by a relative error of at most 0.0041.
Values sent between devices are 32-bit elements; how exact they have to be, the bound alone decides.
No kernel may reach another device: no remote copies, remote signals or barrier semaphores. Data moves between devices by JAX's collectives and lax.ppermute only.
A program may use at most 64 MiB of HBM per device.

v0:
```python
import jax
import jax.numpy as jnp
from jax import lax
from jax.sharding import PartitionSpec as P

ITERS = 2


STEP_SCALE = 0.5
PENALTY = 40.0
EPSILON = 1e-06


def shrink(trial, squares, step_part):
    norms = jnp.sqrt(squares + EPSILON)
    factor = jnp.maximum(0.0, 1.0 - PENALTY * step_part / norms)
    return trial * factor[:, None]


def shards(library, responses, coefficients):
    sample_count = library.shape[0] * lax.axis_size("samp")
    column_sq = lax.psum(jnp.sum(jnp.square(library.astype(jnp.float32)), axis=0), "samp")
    step_sizes = STEP_SCALE * sample_count / column_sq
    moved = coefficients
    for turn in range(ITERS):
        weights_bf = moved.astype(jnp.bfloat16)
        residual = (
            jnp.dot(library, weights_bf, preferred_element_type=jnp.float32)
            - responses.astype(jnp.float32)
        ).astype(jnp.bfloat16)
        local_corr = lax.dot_general(
            library, residual, (((0,), (0,)), ((), ())), preferred_element_type=jnp.float32
        )
        gradient = lax.psum(local_corr, "samp") / sample_count
        trial = moved - step_sizes[:, None] * gradient
        squares = lax.psum(jnp.sum(trial * trial, axis=1), "reg")
        moved = shrink(trial, squares, step_sizes)
    return moved


def solution(mesh):
    return jax.shard_map(
        shards,
        mesh=mesh,
        in_specs=(P("samp", None), P("samp", "reg"), P(None, "reg")),
        out_specs=P(None, "reg"),
        check_vma=False,
    )
```

profile of v0, /device:TPU:32, one launch (start us, length us, event | category | flops | bytes accessed | tf_op | source)
XLA Modules:
  0.0 353.2 jit_solution(14076559235661708130)
XLA Ops:
  6.5 0.0 copy-start.1
  6.5 0.0 all-reduce.3.cloned.1.call-start
  6.5 9.6 %convolution_bitcast_fusion.2 = f32[1024,128]{0,1:T(8,128)} fusion(bf16[3072,1024]{1,0:T(8,128)(2,1)} %param.3, bf16[3072,128]{1,0:T(8,128)(2,1)} %param.4, f32[1024,128]{1,0:T(8,128)} %param.5), kind=kOutput, calls=%fused_computation.7 | convolution fusion | flops 1611923456 | bytes 8126464 | tf_op jit(solution)/shard_map/dot_general | solution.py:31
  16.2 0.0 copy-start
  16.2 0.0 all-reduce.3.cloned.1.call-update
  16.2 0.0 all-reduce.5.cloned.1.call-start
  16.2 0.0 copy-done.1
  16.3 0.2 copy.4
  16.5 4.1 %multiply_reduce_fusion = f32[1024]{0:T(1024)S(1)} fusion(bf16[3072,1024]{1,0:T(8,128)(2,1)} %param.3), kind=kLoop, calls=%fused_computation | loop fusion | flops 9436160 | bytes 6295552 | tf_op jit(solution)/shard_map/reduce_sum | solution.py:22
  20.5 73.5 %psum.36 = f32[1024]{0:T(1024)S(1)} all-reduce(f32[1024]{0:T(1024)S(1)} %multiply_reduce_fusion), channel_id=1, replica_groups=mesh['samp'=32,'reg'=8] {'samp'}, use_global_device_ids=true, to_apply=%region_2.0 | all-reduce | flops 1024 | bytes 8192 | tf_op jit(solution)/shard_map/psum | solution.py:22
  94.0 71.4 %all-reduce.3.cloned.1.call-done = f32[1024,128]{0,1:T(8,128)} async-done(((f32[1024,128]{0,1:T(8,128)}), f32[1024,128]{0,1:T(8,128)}) %all-reduce.3.cloned.1.call-update) | async-done | bytes 524304 | tf_op jit(solution)/shard_map/psum | solution.py:34
  165.4 1.1 multiply_reduce_fusion.2
  166.5 12.4 %psum.37 = f32[1024]{0:T(1024)S(1)} all-reduce(f32[1024]{0:T(1024)S(1)} %get-tuple-element.5), channel_id=1, replica_groups=mesh['samp'=32,'reg'=8] {'reg'}, use_global_device_ids=true, to_apply=%region_4.0 | all-reduce | flops 1024 | bytes 8192 | tf_op jit(solution)/shard_map/psum | solution.py:36
  178.9 0.0 copy-done
  179.0 9.4 %convolution_bitcast_fusion.1 = f32[1024,128]{0,1:T(8,128)} fusion(bf16[3072,1024]{1,0:T(8,128)(2,1)} %param.3, bf16[3072,128]{1,0:T(8,128)(2,1)S(1)} %copy-done, f32[1024,128]{0,1:T(8,128)S(1)} %get-tuple-element.6, f32[1024]{0:T(1024)S(1)} %subtract_maximum_fusion.1), kind=kOutput, calls=%fused_computation.6 | convolution fusion | flops 1612054528 | bytes 8130560 | tf_op jit(solution)/shard_map/dot_general | solution.py:31
  188.3 0.0 all-reduce.5.cloned.1.call-update
  188.3 142.3 %all-reduce.5.cloned.1.call-done = f32[1024,128]{0,1:T(8,128)} async-done(((f32[1024,128]{0,1:T(8,128)}), f32[1024,128]{0,1:T(8,128)}) %all-reduce.5.cloned.1.call-update) | async-done | bytes 524304 | tf_op jit(solution)/shard_map/psum | solution.py:34
  330.7 1.2 multiply_reduce_fusion.1
  331.8 12.4 %psum.39 = f32[1024]{0:T(1024)S(1)} all-reduce(f32[1024]{0:T(1024)S(1)} %multiply_reduce_fusion.1), channel_id=1, replica_groups=mesh['samp'=32,'reg'=8] {'reg'}, use_global_device_ids=true, to_apply=%region_7.0 | all-reduce | flops 1024 | bytes 8192 | tf_op jit(solution)/shard_map/psum | solution.py:36
  344.3 1.1 broadcast_multiply_fusion
  345.4 1.0 copy.5
  (3 shorter events, 0.0 us)
Async XLA Ops:
  6.5 9.7 %copy-start.1 = (f32[1024,128]{1,0:T(8,128)S(1)}, f32[1024,128]{1,0:T(8,128)}, u32[]{:S(2)}) copy-start(f32[1024,128]{1,0:T(8,128)} %param.5) | copy-start | bytes 1572868
  6.5 158.8 %all-reduce.3.cloned.1.call-start = ((), (), s32[]{:S(2)}) async-start(), calls=%async_computation | async-start | bytes 1048576 | tf_op jit(solution)/shard_map/psum | solution.py:34
  16.2 162.8 %copy-start = (bf16[3072,128]{1,0:T(8,128)(2,1)S(1)}, bf16[3072,128]{1,0:T(8,128)(2,1)}, u32[]{:S(2)}) copy-start(bf16[3072,128]{1,0:T(8,128)(2,1)} %param.4) | copy-start | bytes 2359300
  16.2 314.5 %all-reduce.5.cloned.1.call-start = ((), (), s32[]{:S(2)}) async-start(), calls=%async_computation.1 | async-start | bytes 1048576 | tf_op jit(solution)/shard_map/psum | solution.py:34
Sparse Core Ops, SparseCore 0:
  16.3 149.0 all-reduce.2
  188.5 142.1 all-reduce.4
where the time goes:
time: 356 us; the launch traced here: 353 us
  waiting for transfers between devices  214 us (60%)
  blocking collectives  98.3 us (28%)
  matrix products  19 us (5%)
  between operations  13.4 us (4%)
  other arithmetic  7.54 us (2%)
    psum x2, waiting for transfers between devices, shards(): gradient = lax.psum(local_corr, 'samp') / sample_count  214 us
    psum x1, blocking collectives, shards(): lax.psum(jnp.sum(jnp.square(library.astype(jnp.float32)), axis=0), 'samp')  73.5 us
    psum x2, blocking collectives, shards(): squares = lax.psum(jnp.sum(trial * trial, axis=1), 'reg')  24.9 us
    dot_general x2, matrix products, shards(): lax.dot_general(library, residual, (((0,), (0,)), ((), ())), preferred_el...  19 us
  transfers between devices with their start and end apart: 2, of which 2 were waited for; matrix products, arithmetic and copies ran while one was open for 1% of the time, Pallas kernels for 0%

commit v1 on v0

v1 whole, which is shorter than its diff:
```python
import jax
import jax.numpy as jnp
from jax import lax
from jax.experimental import pallas as pl
from jax.experimental.pallas import tpu as pltpu
from jax.sharding import PartitionSpec as P

STEP_SCALE = 0.5
PENALTY = 40.0
EPSILON = 1e-06
LANES = 128
F32 = jnp.float32
BF16 = jnp.bfloat16
VMEM_LIMIT = 48 << 20


def params():
    return pltpu.CompilerParams(vmem_limit_bytes=VMEM_LIMIT)


def to_column(row, first, rows):
    lane = lax.broadcasted_iota(jnp.int32, (rows, LANES), 1)
    own = lax.broadcasted_iota(jnp.int32, (rows, LANES), 0) + first
    return jnp.sum(jnp.where(lane == own, row, 0.0), axis=1, keepdims=True)


def to_row(column):
    rows = column.shape[0]
    lane = lax.broadcasted_iota(jnp.int32, (rows, LANES), 1)
    own = lax.broadcasted_iota(jnp.int32, (rows, LANES), 0)
    return jnp.sum(jnp.where(lane == own, column, 0.0), axis=0, keepdims=True)


def correlate_kernel(place, lib, lib_cols, resp, coef, out, acc, squares):
    step, last = pl.program_id(0), pl.num_programs(0) - 1
    block = lib[...]
    residual = (
        jnp.dot(block, coef[...].astype(BF16), preferred_element_type=F32)
        - resp[...].astype(F32)
    ).astype(BF16)
    right = jnp.concatenate([residual, lib_cols[...]], axis=1)
    part = lax.dot_general(block, right, (((0,), (0,)), ((), ())), preferred_element_type=F32)
    wide = block.astype(F32)
    part_sq = jnp.sum((wide * wide).reshape(-1, 8, wide.shape[1]), axis=0)

    @pl.when(step == 0)
    def _():
        acc[...] = part
        squares[...] = part_sq

    @pl.when(step > 0)
    def _():
        acc[...] += part
        squares[...] += part_sq

    @pl.when(step == last)
    def _():
        chunks = 32
        rows = acc.shape[0] // chunks
        tall = 2 * rows + 1
        column_sq = jnp.sum(squares[...], axis=0, keepdims=True)
        for c in range(chunks):
            out[c * tall:c * tall + rows, :] = acc[c * rows:(c + 1) * rows, :LANES]
            out[c * tall + rows:c * tall + 2 * rows, :] = acc[c * rows:(c + 1) * rows, LANES:]
            at = c * rows // LANES * LANES
            out[c * tall + 2 * rows:(c + 1) * tall, :] = column_sq[:, at:at + LANES]


def correlate(place, library, responses, coefficients, block=512):
    samples, terms = library.shape
    return pl.pallas_call(
        correlate_kernel,
        out_shape=jax.ShapeDtypeStruct((2 * terms + 32, LANES), F32),
        grid_spec=pltpu.PrefetchScalarGridSpec(
            num_scalar_prefetch=1,
            grid=(samples // block,),
            in_specs=[
                pl.BlockSpec((block, terms), lambda i, place: (i, 0)),
                pl.BlockSpec((block, LANES), lambda i, place: (i, place[1])),
                pl.BlockSpec((block, LANES), lambda i, place: (i, 0)),
                pl.BlockSpec((terms, LANES), lambda i, place: (0, 0)),
            ],
            out_specs=pl.BlockSpec((2 * terms + 32, LANES), lambda i, place: (0, 0)),
            scratch_shapes=[
                pltpu.VMEM((terms, 2 * LANES), F32),
                pltpu.VMEM((8, terms), F32),
            ],
        ),
        compiler_params=params(),
        name="correlate",
    )(place, library, library, responses, coefficients)


def first_step_kernel(place, parts, coef, send, state, *, rows, samples):
    tall = 2 * rows + 1
    total = parts[0:2 * rows, :]
    column_sq = parts[2 * rows:tall, :]
    for c in range(1, parts.shape[0] // tall):
        total += parts[c * tall:c * tall + 2 * rows, :]
        column_sq += parts[c * tall + 2 * rows:(c + 1) * tall, :]
    step = STEP_SCALE * samples / to_column(column_sq, place[0] * rows % LANES, rows)
    corr, gram = total[:rows], total[rows:]
    trial = coef[...] - step * (corr / samples)
    squares = to_row(jnp.sum(trial * trial, axis=1, keepdims=True))
    for c in range(8):
        send[c * (rows + 1):c * (rows + 1) + rows, :] = gram
        send[c * (rows + 1) + rows:(c + 1) * (rows + 1), :] = squares
    state[0:rows, :] = trial
    state[rows:2 * rows, :] = corr
    state[2 * rows:3 * rows, :] = jnp.broadcast_to(step, (rows, LANES))


def shrink(trial, squares, step):
    norms = jnp.sqrt(squares + EPSILON)
    return trial * jnp.maximum(0.0, 1.0 - PENALTY * step / norms)


def first_shrink_kernel(gathered, state, moved, *, rows):
    squares = gathered[rows:rows + 1, :]
    for c in range(1, 8):
        squares += gathered[c * (rows + 1) + rows:(c + 1) * (rows + 1), :]
    own = shrink(state[0:rows, :], to_column(squares, 0, rows), state[2 * rows:3 * rows, :])
    for c in range(32):
        moved[c * rows:(c + 1) * rows, :] = own


def second_step_kernel(moved, coef, gathered, state, own, send, trial_out, *, rows, samples):
    change = moved[...].astype(BF16).astype(F32) - coef[...].astype(BF16).astype(F32)
    corr = state[rows:2 * rows, :]
    for c in range(8):
        corr += jnp.dot(
            gathered[c * (rows + 1):c * (rows + 1) + rows, :],
            change[c * LANES:(c + 1) * LANES, :],
            precision=lax.Precision.HIGHEST,
            preferred_element_type=F32,
        )
    trial = own[...] - state[2 * rows:3 * rows, :] * (corr / samples)
    squares = to_row(jnp.sum(trial * trial, axis=1, keepdims=True))
    send[...] = jnp.broadcast_to(squares, (8, LANES))
    trial_out[...] = trial


def second_shrink_kernel(squares, trial, state, moved, *, rows):
    total = jnp.sum(squares[...], axis=0, keepdims=True)
    own = shrink(trial[...], to_column(total, 0, rows), state[2 * rows:3 * rows, :])
    for c in range(32):
        moved[c * rows:(c + 1) * rows, :] = own


def whole(kernel, name, out_shapes, *arrays, **fixed):
    return pl.pallas_call(
        lambda *refs: kernel(*refs, **fixed),
        out_shape=[jax.ShapeDtypeStruct(s, F32) for s in out_shapes],
        compiler_params=params(),
        name=name,
    )(*arrays)


def exchange(array, axis, count):
    blocks = array.reshape(count, array.shape[0] // count, 1, LANES)
    return lax.all_to_all(blocks, axis, 0, 0).reshape(array.shape)


def shards(library, responses, coefficients):
    n_samp, n_reg = lax.axis_size("samp"), lax.axis_size("reg")
    samples, terms = library.shape[0] * n_samp, library.shape[1]
    rows = terms // n_samp
    place = jnp.stack([lax.axis_index("samp"), lax.axis_index("reg")]).astype(jnp.int32)

    parts = correlate(place, library, responses, coefficients)
    parts = exchange(parts, "samp", n_samp)

    send, state = pl.pallas_call(
        lambda *refs: first_step_kernel(*refs, rows=rows, samples=samples),
        out_shape=[
            jax.ShapeDtypeStruct((n_reg * (rows + 1), LANES), F32),
            jax.ShapeDtypeStruct((3 * rows, LANES), F32),
        ],
        grid_spec=pltpu.PrefetchScalarGridSpec(
            num_scalar_prefetch=1,
            grid=(1,),
            in_specs=[
                pl.BlockSpec(parts.shape, lambda i, place: (0, 0)),
                pl.BlockSpec((rows, LANES), lambda i, place: (place[0], 0)),
            ],
            out_specs=[
                pl.BlockSpec((n_reg * (rows + 1), LANES), lambda i, place: (0, 0)),
                pl.BlockSpec((3 * rows, LANES), lambda i, place: (0, 0)),
            ],
        ),
        compiler_params=params(),
        name="first_step",
    )(place, parts, coefficients)
    gathered = exchange(send, "reg", n_reg)

    (spread,) = whole(first_shrink_kernel, "first_shrink", [(terms, LANES)], gathered, state, rows=rows)
    own = spread[:rows]
    moved = exchange(spread, "samp", n_samp)

    send, trial = whole(
        second_step_kernel, "second_step", [(n_reg, LANES), (rows, LANES)],
        moved, coefficients, gathered, state, own, rows=rows, samples=samples,
    )
    squares = exchange(send, "reg", n_reg)
    (spread,) = whole(
        second_shrink_kernel, "second_shrink", [(terms, LANES)], squares, trial, state, rows=rows
    )
    return exchange(spread, "samp", n_samp)


def solution(mesh):
    return jax.shard_map(
        shards,
        mesh=mesh,
        in_specs=(P("samp", None), P("samp", "reg"), P(None, "reg")),
        out_specs=P(None, "reg"),
        check_vma=False,
    )
```

time: 356 us -> 120 us (0.34)
  waiting for transfers between devices: 214 us -> 17.1 us
  matrix products: 19 us -> 0 us
  blocking collectives: 98.3 us -> 81.4 us
  between operations: 13.4 us -> 0.04 us
  Pallas kernels: 0 us -> 12.8 us
  other arithmetic: 7.54 us -> 0.07 us
  starting transfers between devices: 0.04 us -> 4.83 us
    psum x2 -> x0, waiting for transfers between devices: 214 us -> none  [shards(): gradient = lax.psum(local_corr, 'samp') / sample_count]
    psum x3 -> x0, blocking collectives: 98.3 us -> none  [the longest x1 73.5 us: shards(): lax.psum(jnp.sum(jnp.square(library.astype(jnp.float32)), axis=0), 'samp')]
    all_to_all x0 -> x4, blocking collectives: none -> 81.4 us  [exchange(): return lax.all_to_all(blocks, axis, 0, 0).reshape(array.shape)]
    dot_general x2 -> x0, matrix products: 19 us -> none  [shards(): lax.dot_general(library, residual, (((0,), (0,)), ((), ())), preferred_el...]
    all_to_all x0 -> x1, waiting for transfers between devices: none -> 17.1 us  [exchange(): return lax.all_to_all(blocks, axis, 0, 0).reshape(array.shape)]
    pallas_call x0 -> x5, Pallas kernels: none -> 12.8 us  [the longest x1 10.4 us: correlate(): pl.pallas_call(correlate_kernel, out_shape=jax.ShapeDtypeStruct((2 * term...]
    reduce_sum x3 -> x0, other arithmetic: 6.37 us -> none  [the longest x1 4.08 us: shards(): jnp.sum(jnp.square(library.astype(jnp.float32)), axis=0)]
    all_to_all x0 -> x1, starting transfers between devices: none -> 4.83 us  [exchange(): return lax.all_to_all(blocks, axis, 0, 0).reshape(array.shape)]
  transfers between devices with their start and end apart: 2 -> 1, of which waited for: 2 -> 1; matrix products, arithmetic and copies ran while one was open for 1% -> 1% of each run, Pallas kernels for 0% -> 0%
where the time goes in v1:
time: 120 us
  blocking collectives  81.4 us (68%)
  waiting for transfers between devices  17.1 us (14%)
  Pallas kernels  12.8 us (11%)
  starting transfers between devices  4.83 us (4%)
  local copies, waits for them, and re-layouts  3.71 us (3%)
    all_to_all x4, blocking collectives, exchange(): return lax.all_to_all(blocks, axis, 0, 0).reshape(array.shape)  81.4 us
    all_to_all x1, waiting for transfers between devices, exchange(): return lax.all_to_all(blocks, axis, 0, 0).reshape(array.shape)  17.1 us
    pallas_call x1, Pallas kernels, correlate(): pl.pallas_call(correlate_kernel, out_shape=jax.ShapeDtypeStruct((2 * term...  10.4 us
    all_to_all x1, starting transfers between devices, exchange(): return lax.all_to_all(blocks, axis, 0, 0).reshape(array.shape)  4.83 us
    unnamed x7, local copies, waits for them, and re-layouts  2.97 us
  transfers between devices with their start and end apart: 1, of which 1 were waited for; matrix products, arithmetic and copies ran while one was open for 1% of the time, Pallas kernels for 0%

profile of v1, /device:TPU:32, one launch (start us, length us, event | category | flops | bytes accessed | tf_op | source)
XLA Modules:
  0.0 120.0 jit_solution(184195694021180433)
XLA Ops:
  0.0 0.1 pad_add_fusion.place.refs_0_
  0.1 0.0 copy-start
  0.1 1.0 copy-done
  1.1 0.0 copy-start.2
  1.1 1.1 copy-done.2
  2.3 10.4 %correlate.1 = f32[2080,128]{1,0:T(8,128)S(1)} custom-call(s32[2]{0:T(128)S(1)} %pad_add_fusion.place.refs_0_, bf16[3072,1024]{1,0:T(8,128)(2,1)} %lib_cols.1, bf16[3072,1024]{1,0:T(8,128)(2,1)} %lib_cols.1, bf16[3072,128]{1,0:T(8,128)(2,1)S(1)} %copy-done.2, f32[1024,128]{1,0:T(8,128)S(1)} %copy-done), custom_call_target="tpu_custom_call" | custom-call | tf_op jit(solution)/shard_map/correlate/pallas_call | solution.py:71
  12.6 0.0 copy-start.1
  12.6 41.0 %all_to_all.25 = f32[32,65,1,128]{3,2,1,0:T(1,128)S(1)} all-to-all(f32[32,65,1,128]{3,2,1,0:T(1,128)S(1)} %bitcast.18), channel_id=1, replica_groups=mesh['samp'=32,'reg'=8] {'samp'}, dimensions={0} | all-to-all | bytes 2129920 | tf_op jit(solution)/shard_map/all_to_all | solution.py:161
  53.7 0.0 copy-done.1
  53.7 0.7 first_step.1
  54.4 10.4 %all_to_all.26 = f32[8,33,1,128]{3,2,1,0:T(1,128)S(1)} all-to-all(f32[8,33,1,128]{3,2,1,0:T(1,128)S(1)} %bitcast.24), channel_id=1, replica_groups=mesh['samp'=32,'reg'=8] {'reg'}, dimensions={0} | all-to-all | bytes 270336 | tf_op jit(solution)/shard_map/all_to_all | solution.py:161
  64.9 1.0 first_shrink.1
  65.8 4.8 %all-to-all-start.2 = ((f32[32,32,1,128]{3,1,2,0:T(8,128)}), f32[32,32,1,128]{3,1,2,0:T(8,128)S(1)}, u32[]{:S(2)}, u32[]{:S(2)}) async-start(f32[32,32,1,128]{3,1,2,0:T(8,128)} %bitcast.7), calls=%async_computation.2 | async-start | bytes 1048576 | tf_op jit(solution)/shard_map/all_to_all | solution.py:161
  70.7 0.7 slice.4.refs_4_
  71.4 17.1 %all-to-all-done.2 = f32[32,32,1,128]{3,1,2,0:T(8,128)S(1)} async-done(((f32[32,32,1,128]{3,1,2,0:T(8,128)}), f32[32,32,1,128]{3,1,2,0:T(8,128)S(1)}, u32[]{:S(2)}, u32[]{:S(2)}) %all-to-all-start.2) | async-done | bytes 524320 | tf_op jit(solution)/shard_map/all_to_all | solution.py:161
  88.5 0.6 second_step.1
  89.1 7.6 %all_to_all.27 = f32[8,1,1,128]{3,2,1,0:T(1,128)S(1)} all-to-all(f32[8,1,1,128]{3,2,1,0:T(1,128)S(1)} %bitcast.26), channel_id=1, replica_groups=mesh['samp'=32,'reg'=8] {'reg'}, dimensions={0} | all-to-all | bytes 8192 | tf_op jit(solution)/shard_map/all_to_all | solution.py:161
  96.7 0.2 second_shrink.1
  96.9 22.3 %all_to_all.28 = f32[32,32,1,128]{3,1,2,0:T(8,128)S(1)} all-to-all(f32[32,32,1,128]{3,1,2,0:T(8,128)S(1)} %bitcast.21), channel_id=1, replica_groups=mesh['samp'=32,'reg'=8] {'samp'}, dimensions={0} | all-to-all | bytes 1048576 | tf_op jit(solution)/shard_map/all_to_all | solution.py:161
  119.2 0.8 copy.10
Async XLA Ops:
  0.1 1.0 copy-start
  1.1 1.1 copy-start.2
  12.6 41.1 %copy-start.1 = (f32[1024,128]{1,0:T(8,128)S(1)}, f32[1024,128]{1,0:T(8,128)}, u32[]{:S(2)}) copy-start(f32[1024,128]{1,0:T(8,128)} %refs_1_.1) | copy-start | bytes 1572868
  65.8 22.6 %all-to-all-start.2 = ((f32[32,32,1,128]{3,1,2,0:T(8,128)}), f32[32,32,1,128]{3,1,2,0:T(8,128)S(1)}, u32[]{:S(2)}, u32[]{:S(2)}) async-start(f32[32,32,1,128]{3,1,2,0:T(8,128)} %bitcast.7), calls=%async_computation.2 | async-start | bytes 1048576 | tf_op jit(solution)/shard_map/all_to_all | solution.py:161

commit v2 on v1

--- a/solution.py
+++ b/solution.py
@@ -12,6 +12,8 @@
 F32 = jnp.float32
 BF16 = jnp.bfloat16
 VMEM_LIMIT = 48 << 20
+AHEAD = 2
+N_X = 4
 
 
 def params():
@@ -31,64 +33,96 @@
     return jnp.sum(jnp.where(lane == own, column, 0.0), axis=0, keepdims=True)
 
 
-def correlate_kernel(place, lib, lib_cols, resp, coef, out, acc, squares):
-    step, last = pl.program_id(0), pl.num_programs(0) - 1
-    block = lib[...]
-    residual = (
-        jnp.dot(block, coef[...].astype(BF16), preferred_element_type=F32)
-        - resp[...].astype(F32)
-    ).astype(BF16)
-    right = jnp.concatenate([residual, lib_cols[...]], axis=1)
-    part = lax.dot_general(block, right, (((0,), (0,)), ((), ())), preferred_element_type=F32)
-    wide = block.astype(F32)
-    part_sq = jnp.sum((wide * wide).reshape(-1, 8, wide.shape[1]), axis=0)
-
-    @pl.when(step == 0)
-    def _():
-        acc[...] = part
-        squares[...] = part_sq
-
-    @pl.when(step > 0)
-    def _():
-        acc[...] += part
-        squares[...] += part_sq
-
-    @pl.when(step == last)
-    def _():
-        chunks = 32
-        rows = acc.shape[0] // chunks
-        tall = 2 * rows + 1
-        column_sq = jnp.sum(squares[...], axis=0, keepdims=True)
-        for c in range(chunks):
-            out[c * tall:c * tall + rows, :] = acc[c * rows:(c + 1) * rows, :LANES]
-            out[c * tall + rows:c * tall + 2 * rows, :] = acc[c * rows:(c + 1) * rows, LANES:]
-            at = c * rows // LANES * LANES
-            out[c * tall + 2 * rows:(c + 1) * tall, :] = column_sq[:, at:at + LANES]
-
-
-def correlate(place, library, responses, coefficients, block=512):
+def correlate_kernel(place, lib_hbm, resp_hbm, coef_hbm, out, lib, resp, coef, acc, squares, sems, *, blocks, chunks):
+    count = len(blocks)
+    starts = [sum(blocks[:i]) for i in range(count)]
+    copies = [
+        pltpu.make_async_copy(lib_hbm.at[pl.ds(at, size)], lib.at[pl.ds(at, size)], sems.at[i])
+        for i, (at, size) in enumerate(zip(starts, blocks))
+    ]
+    copy_coef = pltpu.make_async_copy(coef_hbm, coef, sems.at[count])
+    copy_resp = pltpu.make_async_copy(resp_hbm, resp, sems.at[count + 1])
+    copy_coef.start()
+    for i in range(AHEAD):
+        copies[i].start()
+    copy_resp.start()
+    copy_coef.wait()
+    weights = coef[...].astype(BF16)
+    own = pl.multiple_of(place[1] * LANES, LANES)
+    residuals = {}
+
+    def residual(i):
+        copies[i].wait()
+        if i + AHEAD < count:
+            copies[i + AHEAD].start()
+        if i == 0:
+            copy_resp.wait()
+        at = pl.ds(starts[i], blocks[i])
+        fit = jnp.dot(lib[at, :], weights, preferred_element_type=F32)
+        residuals[i] = (fit - resp[at, :].astype(F32)).astype(BF16)
+
+    def correlation(i):
+        at = pl.ds(starts[i], blocks[i])
+        block = lib[at, :]
+        right = jnp.concatenate([residuals[i], lib[at, pl.ds(own, LANES)]], axis=1)
+        part = lax.dot_general(block, right, (((0,), (0,)), ((), ())), preferred_element_type=F32)
+        wide = block.astype(F32)
+        part_sq = jnp.sum((wide * wide).reshape(-1, 8, wide.shape[1]), axis=0)
+        if i == 0:
+            acc[...] = part
+            squares[...] = part_sq
+        else:
+            acc[...] += part
+            squares[...] += part_sq
+
+    for i in range(count):
+        residual(i)
+        if i > 0:
+            correlation(i - 1)
+    correlation(count - 1)
+
+    rows = acc.shape[0] // chunks
+    tall = 2 * rows + 1
+    column_sq = jnp.sum(squares[...], axis=0, keepdims=True)
+    for c in range(chunks):
+        out[c * tall:c * tall + rows, :] = acc[c * rows:(c + 1) * rows, :LANES]
+        out[c * tall + rows:c * tall + 2 * rows, :] = acc[c * rows:(c + 1) * rows, LANES:]
+        at = c * rows // LANES * LANES
+        out[c * tall + 2 * rows:(c + 1) * tall, :] = column_sq[:, at:at + LANES]
+
+
+def block_sizes(samples):
+    unit = samples // 12
+    return (unit, unit, 2 * unit, 4 * unit, 4 * unit)
+
+
+def correlate(place, library, responses, coefficients, chunks):
     samples, terms = library.shape
+    blocks = block_sizes(samples)
+    hbm = pl.BlockSpec(memory_space=pltpu.HBM)
     return pl.pallas_call(
-        correlate_kernel,
-        out_shape=jax.ShapeDtypeStruct((2 * terms + 32, LANES), F32),
-        grid_spec=pltpu.PrefetchScalarGridSpec(
-            num_scalar_prefetch=1,
-            grid=(samples // block,),
-            in_specs=[
-                pl.BlockSpec((block, terms), lambda i, place: (i, 0)),
-                pl.BlockSpec((block, LANES), lambda i, place: (i, place[1])),
-                pl.BlockSpec((block, LANES), lambda i, place: (i, 0)),
-                pl.BlockSpec((terms, LANES), lambda i, place: (0, 0)),
-            ],
-            out_specs=pl.BlockSpec((2 * terms + 32, LANES), lambda i, place: (0, 0)),
-            scratch_shapes=[
-                pltpu.VMEM((terms, 2 * LANES), F32),
-                pltpu.VMEM((8, terms), F32),
-            ],
-        ),
+        lambda *refs: correlate_kernel(*refs, blocks=blocks, chunks=chunks),
+        out_shape=jax.ShapeDtypeStruct((2 * terms + chunks, LANES), F32),
+        in_specs=[pl.BlockSpec(memory_space=pltpu.SMEM), hbm, hbm, hbm],
+        scratch_shapes=[
+            pltpu.VMEM((samples, terms), BF16),
+            pltpu.VMEM((samples, LANES), BF16),
+            pltpu.VMEM((terms, LANES), F32),
+            pltpu.VMEM((terms, 2 * LANES), F32),
+            pltpu.VMEM((8, terms), F32),
+            pltpu.SemaphoreType.DMA((len(blocks) + 2,)),
+        ],
         compiler_params=params(),
         name="correlate",
-    )(place, library, library, responses, coefficients)
+    )(place, library, responses, coefficients)
+
+
+def add_kernel(parts, out):
+    tall = out.shape[0]
+    total = parts[0:tall, :]
+    for c in range(1, parts.shape[0] // tall):
+        total += parts[c * tall:(c + 1) * tall, :]
+    out[...] = total
 
 
 def first_step_kernel(place, parts, coef, send, state, *, rows, samples):
@@ -115,11 +149,12 @@
     return trial * jnp.maximum(0.0, 1.0 - PENALTY * step / norms)
 
 
-def first_shrink_kernel(gathered, state, moved, *, rows):
+def first_shrink_kernel(gathered, state, moved, own_out, *, rows):
     squares = gathered[rows:rows + 1, :]
     for c in range(1, 8):
         squares += gathered[c * (rows + 1) + rows:(c + 1) * (rows + 1), :]
     own = shrink(state[0:rows, :], to_column(squares, 0, rows), state[2 * rows:3 * rows, :])
+    own_out[...] = own
     for c in range(32):
         moved[c * rows:(c + 1) * rows, :] = own
 
@@ -156,9 +191,9 @@
     )(*arrays)
 
 
-def exchange(array, axis, count):
+def exchange(array, axis, count, groups=None):
     blocks = array.reshape(count, array.shape[0] // count, 1, LANES)
-    return lax.all_to_all(blocks, axis, 0, 0).reshape(array.shape)
+    return lax.all_to_all(blocks, axis, 0, 0, axis_index_groups=groups).reshape(array.shape)
 
 
 def shards(library, responses, coefficients):
@@ -167,8 +202,13 @@
     rows = terms // n_samp
     place = jnp.stack([lax.axis_index("samp"), lax.axis_index("reg")]).astype(jnp.int32)
 
-    parts = correlate(place, library, responses, coefficients)
-    parts = exchange(parts, "samp", n_samp)
+    n_z = n_samp // N_X
+    over_x = [[x * n_z + z for x in range(N_X)] for z in range(n_z)]
+    over_z = [[x * n_z + z for z in range(n_z)] for x in range(N_X)]
+    parts = correlate(place, library, responses, coefficients, n_samp)
+    parts = exchange(parts, "samp", N_X, over_x)
+    (parts,) = whole(add_kernel, "add", [(parts.shape[0] // N_X, LANES)], parts)
+    parts = exchange(parts, "samp", n_z, over_z)
 
     send, state = pl.pallas_call(
         lambda *refs: first_step_kernel(*refs, rows=rows, samples=samples),
@@ -193,8 +233,9 @@
     )(place, parts, coefficients)
     gathered = exchange(send, "reg", n_reg)
 
-    (spread,) = whole(first_shrink_kernel, "first_shrink", [(terms, LANES)], gathered, state, rows=rows)
-    own = spread[:rows]
+    spread, own = whole(
+        first_shrink_kernel, "first_shrink", [(terms, LANES), (rows, LANES)], gathered, state, rows=rows
+    )
     moved = exchange(spread, "samp", n_samp)
 
     send, trial = whole(

time: 120 us -> 112 us (0.933)
  blocking collectives: 81.4 us -> 99.5 us
  waiting for transfers between devices: 17.1 us -> 0 us
  starting transfers between devices: 4.83 us -> 0 us
  Pallas kernels: 12.8 us -> 8.97 us
    all_to_all x4 -> x6, blocking collectives: 81.4 us -> 99.5 us  [exchange(): lax.all_to_all(blocks, axis, 0, 0, axis_index_groups=groups)]
    all_to_all x1 -> x0, waiting for transfers between devices: 17.1 us -> none  [exchange(): return lax.all_to_all(blocks, axis, 0, 0).reshape(array.shape)]
    all_to_all x1 -> x0, starting transfers between devices: 4.83 us -> none  [exchange(): return lax.all_to_all(blocks, axis, 0, 0).reshape(array.shape)]
    pallas_call x1, Pallas kernels: 10.4 us -> 7.24 us  [correlate(): pl.pallas_call(lambda *refs: correlate_kernel(*refs, blocks=blocks, chunk...]
  transfers between devices with their start and end apart: 1 -> 0, of which waited for: 1 -> 0; matrix products, arithmetic and copies ran while one was open for 1% -> 0% of each run, Pallas kernels for 0% -> 0%
where the time goes in v2:
time: 112 us
  blocking collectives  99.5 us (89%)
  Pallas kernels  8.97 us (8%)
  local copies, waits for them, and re-layouts  2.97 us (3%)
    all_to_all x6, blocking collectives, exchange(): lax.all_to_all(blocks, axis, 0, 0, axis_index_groups=groups)  99.5 us
    pallas_call x1, Pallas kernels, correlate(): pl.pallas_call(lambda *refs: correlate_kernel(*refs, blocks=blocks, chunk...  7.24 us
    unnamed x7, local copies, waits for them, and re-layouts  2.97 us

profile of v2, /device:TPU:32, one launch (start us, length us, event | category | flops | bytes accessed | tf_op | source)
XLA Modules:
  0.0 111.5 jit_solution(11731796603117251993)
XLA Ops:
  0.0 0.1 pad_add_fusion.refs_0_
  0.1 0.0 copy-start
  0.1 1.0 copy-done
  1.1 0.0 copy-start.2
  1.1 1.1 %copy-done.2 = bf16[3072,128]{1,0:T(8,128)(2,1)S(1)} copy-done((bf16[3072,128]{1,0:T(8,128)(2,1)S(1)}, bf16[3072,128]{1,0:T(8,128)(2,1)}, u32[]{:S(2)}) %copy-start.2) | copy-done | bytes 786456
  2.3 7.2 %correlate.1 = f32[2080,128]{1,0:T(8,128)S(1)} custom-call(s32[2]{0:T(128)S(1)} %pad_add_fusion.refs_0_, bf16[3072,1024]{1,0:T(8,128)(2,1)} %refs_1_.2, bf16[3072,128]{1,0:T(8,128)(2,1)S(1)} %copy-done.2, f32[1024,128]{1,0:T(8,128)S(1)} %copy-done), custom_call_target="tpu_custom_call" | custom-call | tf_op jit(solution)/shard_map/correlate/pallas_call | solution.py:103
  9.5 19.4 %all_to_all.30 = f32[4,520,1,128]{3,1,2,0:T(8,128)S(1)} all-to-all(f32[4,520,1,128]{3,1,2,0:T(8,128)S(1)} %bitcast.22), channel_id=1, replica_groups={{0,64,128,192},{8,72,136,200},{16,80,144,208},{24,88,152,216},{32,96,16..., dimensions={0} | all-to-all | bytes 2129920 | tf_op jit(solution)/shard_map/all_to_all | solution.py:196
  28.9 0.0 copy-start.1
  28.9 17.8 %all_to_all.31 = f32[8,65,1,128]{3,2,1,0:T(1,128)S(1)} all-to-all(f32[8,65,1,128]{3,2,1,0:T(1,128)S(1)} %bitcast.29), channel_id=1, replica_groups={{0,8,16,24,32,40,48,56},{64,72,80,88,96,104,112,120},{128,136,144,152,1..., dimensions={0} | all-to-all | bytes 532480 | tf_op jit(solution)/shard_map/all_to_all | solution.py:196
  46.7 0.0 copy-done.1
  46.7 0.7 first_step.1
  47.5 10.5 %all_to_all.32 = f32[8,33,1,128]{3,2,1,0:T(1,128)S(1)} all-to-all(f32[8,33,1,128]{3,2,1,0:T(1,128)S(1)} %bitcast.31), channel_id=1, replica_groups=mesh['samp'=32,'reg'=8] {'reg'}, dimensions={0} | all-to-all | bytes 270336 | tf_op jit(solution)/shard_map/all_to_all | solution.py:196
  57.9 0.2 first_shrink.1
  58.1 21.9 %all_to_all.33 = f32[32,32,1,128]{3,1,2,0:T(8,128)S(1)} all-to-all(f32[32,32,1,128]{3,1,2,0:T(8,128)S(1)} %bitcast.30), channel_id=1, replica_groups=mesh['samp'=32,'reg'=8] {'samp'}, dimensions={0} | all-to-all | bytes 1048576 | tf_op jit(solution)/shard_map/all_to_all | solution.py:196
  80.0 0.7 second_step.1
  80.6 7.6 %all_to_all.34 = f32[8,1,1,128]{3,2,1,0:T(1,128)S(1)} all-to-all(f32[8,1,1,128]{3,2,1,0:T(1,128)S(1)} %bitcast.33), channel_id=1, replica_groups=mesh['samp'=32,'reg'=8] {'reg'}, dimensions={0} | all-to-all | bytes 8192 | tf_op jit(solution)/shard_map/all_to_all | solution.py:196
  88.3 0.1 second_shrink.1
  88.4 22.3 %all_to_all.35 = f32[32,32,1,128]{3,1,2,0:T(8,128)S(1)} all-to-all(f32[32,32,1,128]{3,1,2,0:T(8,128)S(1)} %bitcast.25), channel_id=1, replica_groups=mesh['samp'=32,'reg'=8] {'samp'}, dimensions={0} | all-to-all | bytes 1048576 | tf_op jit(solution)/shard_map/all_to_all | solution.py:196
  110.7 0.8 copy.11
  (1 shorter events, 0.0 us)
Async XLA Ops:
  0.1 1.0 copy-start
  1.1 1.1 %copy-start.2 = (bf16[3072,128]{1,0:T(8,128)(2,1)S(1)}, bf16[3072,128]{1,0:T(8,128)(2,1)}, u32[]{:S(2)}) copy-start(bf16[3072,128]{1,0:T(8,128)(2,1)} %refs_2_.2) | copy-start | bytes 2359300
  28.9 17.9 %copy-start.1 = (f32[1024,128]{1,0:T(8,128)S(1)}, f32[1024,128]{1,0:T(8,128)}, u32[]{:S(2)}) copy-start(f32[1024,128]{1,0:T(8,128)} %refs_1_.3) | copy-start | bytes 1572868

commit v3 on v2

--- a/solution.py
+++ b/solution.py
@@ -114,7 +114,7 @@
         ],
         compiler_params=params(),
         name="correlate",
-    )(place, library, responses, coefficients)
+    )(place, library, *(pltpu.with_memory_space_constraint(a, pltpu.HBM) for a in (responses, coefficients)))
 
 
 def add_kernel(parts, out):
@@ -125,7 +125,7 @@
     out[...] = total
 
 
-def first_step_kernel(place, parts, coef, send, state, *, rows, samples):
+def first_step_kernel(place, parts, coef, send, gram_out, state, *, rows, samples):
     tall = 2 * rows + 1
     total = parts[0:2 * rows, :]
     column_sq = parts[2 * rows:tall, :]
@@ -136,9 +136,8 @@
     corr, gram = total[:rows], total[rows:]
     trial = coef[...] - step * (corr / samples)
     squares = to_row(jnp.sum(trial * trial, axis=1, keepdims=True))
-    for c in range(8):
-        send[c * (rows + 1):c * (rows + 1) + rows, :] = gram
-        send[c * (rows + 1) + rows:(c + 1) * (rows + 1), :] = squares
+    send[...] = jnp.broadcast_to(squares, send.shape)
+    gram_out[...] = gram
     state[0:rows, :] = trial
     state[rows:2 * rows, :] = corr
     state[2 * rows:3 * rows, :] = jnp.broadcast_to(step, (rows, LANES))
@@ -149,22 +148,20 @@
     return trial * jnp.maximum(0.0, 1.0 - PENALTY * step / norms)
 
 
-def first_shrink_kernel(gathered, state, moved, own_out, *, rows):
-    squares = gathered[rows:rows + 1, :]
-    for c in range(1, 8):
-        squares += gathered[c * (rows + 1) + rows:(c + 1) * (rows + 1), :]
-    own = shrink(state[0:rows, :], to_column(squares, 0, rows), state[2 * rows:3 * rows, :])
+def first_shrink_kernel(squares, state, moved, own_out, *, rows):
+    total = jnp.sum(squares[...], axis=0, keepdims=True)
+    own = shrink(state[0:rows, :], to_column(total, 0, rows), state[2 * rows:3 * rows, :])
     own_out[...] = own
     for c in range(32):
         moved[c * rows:(c + 1) * rows, :] = own
 
 
-def second_step_kernel(moved, coef, gathered, state, own, send, trial_out, *, rows, samples):
+def second_step_kernel(moved, coef, gram, state, own, send, trial_out, *, rows, samples):
     change = moved[...].astype(BF16).astype(F32) - coef[...].astype(BF16).astype(F32)
     corr = state[rows:2 * rows, :]
     for c in range(8):
         corr += jnp.dot(
-            gathered[c * (rows + 1):c * (rows + 1) + rows, :],
+            gram[c * rows:(c + 1) * rows, :],
             change[c * LANES:(c + 1) * LANES, :],
             precision=lax.Precision.HIGHEST,
             preferred_element_type=F32,
@@ -210,10 +207,11 @@
     (parts,) = whole(add_kernel, "add", [(parts.shape[0] // N_X, LANES)], parts)
     parts = exchange(parts, "samp", n_z, over_z)
 
-    send, state = pl.pallas_call(
+    send, gram, state = pl.pallas_call(
         lambda *refs: first_step_kernel(*refs, rows=rows, samples=samples),
         out_shape=[
-            jax.ShapeDtypeStruct((n_reg * (rows + 1), LANES), F32),
+            jax.ShapeDtypeStruct((n_reg, LANES), F32),
+            jax.ShapeDtypeStruct((rows, LANES), F32),
             jax.ShapeDtypeStruct((3 * rows, LANES), F32),
         ],
         grid_spec=pltpu.PrefetchScalarGridSpec(
@@ -224,23 +222,24 @@
                 pl.BlockSpec((rows, LANES), lambda i, place: (place[0], 0)),
             ],
             out_specs=[
-                pl.BlockSpec((n_reg * (rows + 1), LANES), lambda i, place: (0, 0)),
+                pl.BlockSpec((n_reg, LANES), lambda i, place: (0, 0)),
+                pl.BlockSpec((rows, LANES), lambda i, place: (0, 0)),
                 pl.BlockSpec((3 * rows, LANES), lambda i, place: (0, 0)),
             ],
         ),
         compiler_params=params(),
         name="first_step",
     )(place, parts, coefficients)
-    gathered = exchange(send, "reg", n_reg)
-
+    squares = exchange(send, "reg", n_reg)
     spread, own = whole(
-        first_shrink_kernel, "first_shrink", [(terms, LANES), (rows, LANES)], gathered, state, rows=rows
-    )
+        first_shrink_kernel, "first_shrink", [(terms, LANES), (rows, LANES)], squares, state, rows=rows
+    )
+    gram = lax.all_gather(gram, "reg", axis=0, tiled=True)
     moved = exchange(spread, "samp", n_samp)
 
     send, trial = whole(
         second_step_kernel, "second_step", [(n_reg, LANES), (rows, LANES)],
-        moved, coefficients, gathered, state, own, rows=rows, samples=samples,
+        moved, coefficients, gram, state, own, rows=rows, samples=samples,
     )
     squares = exchange(send, "reg", n_reg)
     (spread,) = whole(

time: 112 us -> 111 us (level)
  blocking collectives: 99.5 us -> 89.4 us
  waiting for transfers between devices: 0 us -> 5.23 us
  starting transfers between devices: 0 us -> 5.01 us
  local copies, waits for them, and re-layouts: 2.97 us -> 0.8 us
    all_to_all x6 -> x5, blocking collectives: 99.5 us -> 76.6 us  [exchange(): lax.all_to_all(blocks, axis, 0, 0, axis_index_groups=groups)]
    all_gather x0 -> x1, blocking collectives: none -> 12.8 us  [shards(): gram = lax.all_gather(gram, 'reg', axis=0, tiled=True)]
    all_to_all x0 -> x1, waiting for transfers between devices: none -> 5.23 us  [exchange(): lax.all_to_all(blocks, axis, 0, 0, axis_index_groups=groups)]
    all_to_all x0 -> x1, starting transfers between devices: none -> 5.01 us  [exchange(): lax.all_to_all(blocks, axis, 0, 0, axis_index_groups=groups)]
    unnamed x7 -> x3, local copies, waits for them, and re-layouts: 2.97 us -> 0.8 us
  transfers between devices with their start and end apart: 0 -> 1, of which waited for: 0 -> 1; matrix products, arithmetic and copies ran while one was open for 0% -> 0% of each run, Pallas kernels for 0% -> 0%
where the time goes in v3:
time: 111 us
  blocking collectives  89.4 us (81%)
  Pallas kernels  10 us (9%)
  waiting for transfers between devices  5.23 us (5%)
  starting transfers between devices  5.01 us (5%)
    all_to_all x5, blocking collectives, exchange(): lax.all_to_all(blocks, axis, 0, 0, axis_index_groups=groups)  76.6 us
    all_gather x1, blocking collectives, shards(): gram = lax.all_gather(gram, 'reg', axis=0, tiled=True)  12.8 us
    pallas_call x1, Pallas kernels, correlate(): pl.pallas_call(lambda *refs: correlate_kernel(*refs, blocks=blocks, chunk...  7.5 us
    all_to_all x1, waiting for transfers between devices, exchange(): lax.all_to_all(blocks, axis, 0, 0, axis_index_groups=groups)  5.23 us
    all_to_all x1, starting transfers between devices, exchange(): lax.all_to_all(blocks, axis, 0, 0, axis_index_groups=groups)  5.01 us
  transfers between devices with their start and end apart: 1, of which 1 were waited for; matrix products, arithmetic and copies ran while one was open for 0% of the time, Pallas kernels for 0%

profile of v3, /device:TPU:32, one launch (start us, length us, event | category | flops | bytes accessed | tf_op | source)
XLA Modules:
  0.0 110.5 jit_solution(11315329451797002364)
XLA Ops:
  0.0 0.1 pad_add_fusion.refs_0_
  0.1 7.5 %correlate.1 = f32[2080,128]{1,0:T(8,128)S(1)} custom-call(s32[2]{0:T(128)S(1)} %pad_add_fusion.refs_0_, bf16[3072,1024]{1,0:T(8,128)(2,1)} %refs_1_.2, bf16[3072,128]{1,0:T(8,128)(2,1)} %refs_2_.2, f32[1024,128]{1,0:T(8,128)} %refs_1_.3), custom_call_target="tpu_custom_call" | custom-call | tf_op jit(solution)/shard_map/correlate/pallas_call | solution.py:103
  7.6 19.4 %all_to_all.30 = f32[4,520,1,128]{3,1,2,0:T(8,128)S(1)} all-to-all(f32[4,520,1,128]{3,1,2,0:T(8,128)S(1)} %bitcast.24), channel_id=1, replica_groups={{0,64,128,192},{8,72,136,200},{16,80,144,208},{24,88,152,216},{32,96,16..., dimensions={0} | all-to-all | bytes 2129920 | tf_op jit(solution)/shard_map/all_to_all | solution.py:193
  26.9 0.0 copy-start
  27.0 17.8 %all_to_all.31 = f32[8,65,1,128]{3,2,1,0:T(1,128)S(1)} all-to-all(f32[8,65,1,128]{3,2,1,0:T(1,128)S(1)} %bitcast.29), channel_id=1, replica_groups={{0,8,16,24,32,40,48,56},{64,72,80,88,96,104,112,120},{128,136,144,152,1..., dimensions={0} | all-to-all | bytes 532480 | tf_op jit(solution)/shard_map/all_to_all | solution.py:193
  44.8 0.0 copy-done
  44.8 0.7 first_step.1
  45.5 9.5 %all_to_all.32 = f32[8,1,1,128]{3,2,1,0:T(1,128)S(1)} all-to-all(f32[8,1,1,128]{3,2,1,0:T(1,128)S(1)} %bitcast.32), channel_id=1, replica_groups=mesh['samp'=32,'reg'=8] {'reg'}, dimensions={0} | all-to-all | bytes 8192 | tf_op jit(solution)/shard_map/all_to_all | solution.py:193
  55.1 1.0 first_shrink.1
  56.0 5.0 %all-to-all-start.3 = ((f32[32,32,1,128]{3,1,2,0:T(8,128)}), f32[32,32,1,128]{3,1,2,0:T(8,128)S(1)}, u32[]{:S(2)}, u32[]{:S(2)}) async-start(f32[32,32,1,128]{3,1,2,0:T(8,128)} %bitcast.11), calls=%async_computation.3 | async-start | bytes 1048576 | tf_op jit(solution)/shard_map/all_to_all | solution.py:193
  61.1 12.8 %all_gather.3.refs_2_ = f32[256,128]{1,0:T(8,128)S(1)} all-gather(f32[32,128]{1,0:T(8,128)S(1)} %get-tuple-element.15), channel_id=1, replica_groups=mesh['samp'=32,'reg'=8] {'reg'}, dimensions={0}, use_global_device_ids=true | all-gather | bytes 147456 | tf_op jit(solution)/shard_map/all_gather | solution.py:237
  73.8 5.2 %all-to-all-done.3 = f32[32,32,1,128]{3,1,2,0:T(8,128)S(1)} async-done(((f32[32,32,1,128]{3,1,2,0:T(8,128)}), f32[32,32,1,128]{3,1,2,0:T(8,128)S(1)}, u32[]{:S(2)}, u32[]{:S(2)}) %all-to-all-start.3) | async-done | bytes 524320 | tf_op jit(solution)/shard_map/all_to_all | solution.py:193
  79.0 0.6 second_step.1
  79.7 7.6 %all_to_all.33 = f32[8,1,1,128]{3,2,1,0:T(1,128)S(1)} all-to-all(f32[8,1,1,128]{3,2,1,0:T(1,128)S(1)} %bitcast.33), channel_id=1, replica_groups=mesh['samp'=32,'reg'=8] {'reg'}, dimensions={0} | all-to-all | bytes 8192 | tf_op jit(solution)/shard_map/all_to_all | solution.py:193
  87.3 0.1 second_shrink.1
  87.5 22.3 %all_to_all.34 = f32[32,32,1,128]{3,1,2,0:T(8,128)S(1)} all-to-all(f32[32,32,1,128]{3,1,2,0:T(8,128)S(1)} %bitcast.27), channel_id=1, replica_groups=mesh['samp'=32,'reg'=8] {'samp'}, dimensions={0} | all-to-all | bytes 1048576 | tf_op jit(solution)/shard_map/all_to_all | solution.py:193
  109.7 0.8 copy.11
  (1 shorter events, 0.0 us)
Async XLA Ops:
  26.9 17.9 %copy-start = (f32[1024,128]{1,0:T(8,128)S(1)}, f32[1024,128]{1,0:T(8,128)}, u32[]{:S(2)}) copy-start(f32[1024,128]{1,0:T(8,128)} %refs_1_.3) | copy-start | bytes 1572868
  56.0 23.0 %all-to-all-start.3 = ((f32[32,32,1,128]{3,1,2,0:T(8,128)}), f32[32,32,1,128]{3,1,2,0:T(8,128)S(1)}, u32[]{:S(2)}, u32[]{:S(2)}) async-start(f32[32,32,1,128]{3,1,2,0:T(8,128)} %bitcast.11), calls=%async_computation.3 | async-start | bytes 1048576 | tf_op jit(solution)/shard_map/all_to_all | solution.py:193

commit v4 on v2

--- a/solution.py
+++ b/solution.py
@@ -12,7 +12,6 @@
 F32 = jnp.float32
 BF16 = jnp.bfloat16
 VMEM_LIMIT = 48 << 20
-AHEAD = 2
 N_X = 4
 
 
@@ -36,27 +35,31 @@
 def correlate_kernel(place, lib_hbm, resp_hbm, coef_hbm, out, lib, resp, coef, acc, squares, sems, *, blocks, chunks):
     count = len(blocks)
     starts = [sum(blocks[:i]) for i in range(count)]
-    copies = [
-        pltpu.make_async_copy(lib_hbm.at[pl.ds(at, size)], lib.at[pl.ds(at, size)], sems.at[i])
-        for i, (at, size) in enumerate(zip(starts, blocks))
-    ]
-    copy_coef = pltpu.make_async_copy(coef_hbm, coef, sems.at[count])
-    copy_resp = pltpu.make_async_copy(resp_hbm, resp, sems.at[count + 1])
+    unit = blocks[0]
+
+    def rows_copy(source, target, at, size, sem):
+        return pltpu.make_async_copy(source.at[pl.ds(at, size)], target.at[pl.ds(at, size)], sems.at[sem])
+
+    copy_coef = pltpu.make_async_copy(coef_hbm, coef, sems.at[0])
+    copies = []
+    slot = 1
+    for at, size in zip(starts, blocks):
+        own = [rows_copy(lib_hbm, lib, at + j * unit, unit, slot + j) for j in range(size // unit)]
+        own.append(rows_copy(resp_hbm, resp, at, size, slot + len(own)))
+        slot += len(own)
+        copies.append(own)
     copy_coef.start()
-    for i in range(AHEAD):
-        copies[i].start()
-    copy_resp.start()
+    for own in copies:
+        for copy in own:
+            copy.start()
     copy_coef.wait()
     weights = coef[...].astype(BF16)
-    own = pl.multiple_of(place[1] * LANES, LANES)
+    columns = pl.multiple_of(place[1] * LANES, LANES)
     residuals = {}
 
     def residual(i):
-        copies[i].wait()
-        if i + AHEAD < count:
-            copies[i + AHEAD].start()
-        if i == 0:
-            copy_resp.wait()
+        for copy in copies[i]:
+            copy.wait()
         at = pl.ds(starts[i], blocks[i])
         fit = jnp.dot(lib[at, :], weights, preferred_element_type=F32)
         residuals[i] = (fit - resp[at, :].astype(F32)).astype(BF16)
@@ -64,7 +67,7 @@
     def correlation(i):
         at = pl.ds(starts[i], blocks[i])
         block = lib[at, :]
-        right = jnp.concatenate([residuals[i], lib[at, pl.ds(own, LANES)]], axis=1)
+        right = jnp.concatenate([residuals[i], lib[at, pl.ds(columns, LANES)]], axis=1)
         part = lax.dot_general(block, right, (((0,), (0,)), ((), ())), preferred_element_type=F32)
         wide = block.astype(F32)
         part_sq = jnp.sum((wide * wide).reshape(-1, 8, wide.shape[1]), axis=0)
@@ -93,7 +96,7 @@
 
 def block_sizes(samples):
     unit = samples // 12
-    return (unit, unit, 2 * unit, 4 * unit, 4 * unit)
+    return (unit, 2 * unit, 3 * unit, 3 * unit, 3 * unit)
 
 
 def correlate(place, library, responses, coefficients, chunks):
@@ -110,11 +113,11 @@
             pltpu.VMEM((terms, LANES), F32),
             pltpu.VMEM((terms, 2 * LANES), F32),
             pltpu.VMEM((8, terms), F32),
-            pltpu.SemaphoreType.DMA((len(blocks) + 2,)),
+            pltpu.SemaphoreType.DMA((1 + samples // blocks[0] + len(blocks),)),
         ],
         compiler_params=params(),
         name="correlate",
-    )(place, library, responses, coefficients)
+    )(place, library, *(pltpu.with_memory_space_constraint(a, pltpu.HBM) for a in (responses, coefficients)))
 
 
 def add_kernel(parts, out):

time: 112 us -> 109 us (0.973)
  local copies, waits for them, and re-layouts: 2.97 us -> 0.8 us
    unnamed x7 -> x3, local copies, waits for them, and re-layouts: 2.97 us -> 0.8 us
where the time goes in v4:
time: 109 us
  blocking collectives  99.5 us (91%)
  Pallas kernels  8.62 us (8%)
    all_to_all x6, blocking collectives, exchange(): lax.all_to_all(blocks, axis, 0, 0, axis_index_groups=groups)  99.5 us
    pallas_call x1, Pallas kernels, correlate(): pl.pallas_call(lambda *refs: correlate_kernel(*refs, blocks=blocks, chunk...  6.89 us

profile of v4, /device:TPU:32, one launch (start us, length us, event | category | flops | bytes accessed | tf_op | source)
XLA Modules:
  0.0 109.0 jit_solution(11591535276865840763)
XLA Ops:
  0.0 0.1 pad_add_fusion.refs_0_
  0.1 6.9 %correlate.1 = f32[2080,128]{1,0:T(8,128)S(1)} custom-call(s32[2]{0:T(128)S(1)} %pad_add_fusion.refs_0_, bf16[3072,1024]{1,0:T(8,128)(2,1)} %refs_1_.2, bf16[3072,128]{1,0:T(8,128)(2,1)} %refs_2_.2, f32[1024,128]{1,0:T(8,128)} %refs_1_.3), custom_call_target="tpu_custom_call" | custom-call | tf_op jit(solution)/shard_map/correlate/pallas_call | solution.py:106
  7.0 19.4 %all_to_all.30 = f32[4,520,1,128]{3,1,2,0:T(8,128)S(1)} all-to-all(f32[4,520,1,128]{3,1,2,0:T(8,128)S(1)} %bitcast.22), channel_id=1, replica_groups={{0,64,128,192},{8,72,136,200},{16,80,144,208},{24,88,152,216},{32,96,16..., dimensions={0} | all-to-all | bytes 2129920 | tf_op jit(solution)/shard_map/all_to_all | solution.py:199
  26.3 0.0 copy-start
  26.4 17.8 %all_to_all.31 = f32[8,65,1,128]{3,2,1,0:T(1,128)S(1)} all-to-all(f32[8,65,1,128]{3,2,1,0:T(1,128)S(1)} %bitcast.29), channel_id=1, replica_groups={{0,8,16,24,32,40,48,56},{64,72,80,88,96,104,112,120},{128,136,144,152,1..., dimensions={0} | all-to-all | bytes 532480 | tf_op jit(solution)/shard_map/all_to_all | solution.py:199
  44.2 0.0 copy-done
  44.2 0.7 first_step.1
  44.9 10.5 %all_to_all.32 = f32[8,33,1,128]{3,2,1,0:T(1,128)S(1)} all-to-all(f32[8,33,1,128]{3,2,1,0:T(1,128)S(1)} %bitcast.31), channel_id=1, replica_groups=mesh['samp'=32,'reg'=8] {'reg'}, dimensions={0} | all-to-all | bytes 270336 | tf_op jit(solution)/shard_map/all_to_all | solution.py:199
  55.4 0.2 first_shrink.1
  55.6 21.9 %all_to_all.33 = f32[32,32,1,128]{3,1,2,0:T(8,128)S(1)} all-to-all(f32[32,32,1,128]{3,1,2,0:T(8,128)S(1)} %bitcast.30), channel_id=1, replica_groups=mesh['samp'=32,'reg'=8] {'samp'}, dimensions={0} | all-to-all | bytes 1048576 | tf_op jit(solution)/shard_map/all_to_all | solution.py:199
  77.5 0.7 second_step.1
  78.1 7.6 %all_to_all.34 = f32[8,1,1,128]{3,2,1,0:T(1,128)S(1)} all-to-all(f32[8,1,1,128]{3,2,1,0:T(1,128)S(1)} %bitcast.33), channel_id=1, replica_groups=mesh['samp'=32,'reg'=8] {'reg'}, dimensions={0} | all-to-all | bytes 8192 | tf_op jit(solution)/shard_map/all_to_all | solution.py:199
  85.7 0.1 second_shrink.1
  85.9 22.3 %all_to_all.35 = f32[32,32,1,128]{3,1,2,0:T(8,128)S(1)} all-to-all(f32[32,32,1,128]{3,1,2,0:T(8,128)S(1)} %bitcast.25), channel_id=1, replica_groups=mesh['samp'=32,'reg'=8] {'samp'}, dimensions={0} | all-to-all | bytes 1048576 | tf_op jit(solution)/shard_map/all_to_all | solution.py:199
  108.2 0.8 copy.11
  (1 shorter events, 0.0 us)
Async XLA Ops:
  26.3 17.9 %copy-start = (f32[1024,128]{1,0:T(8,128)S(1)}, f32[1024,128]{1,0:T(8,128)}, u32[]{:S(2)}) copy-start(f32[1024,128]{1,0:T(8,128)} %refs_1_.3) | copy-start | bytes 1572868

commit v5 on v4

--- a/solution.py
+++ b/solution.py
@@ -19,9 +19,12 @@
     return pltpu.CompilerParams(vmem_limit_bytes=VMEM_LIMIT)
 
 
-def to_column(row, first, rows):
+def to_column(row, rows, first=0, run=None):
     lane = lax.broadcasted_iota(jnp.int32, (rows, LANES), 1)
-    own = lax.broadcasted_iota(jnp.int32, (rows, LANES), 0) + first
+    own = lax.broadcasted_iota(jnp.int32, (rows, LANES), 0)
+    if run is not None:
+        own = jnp.where(own < run, own, own - run + LANES // 2)
+        own = jnp.bitwise_and(own + first, LANES - 1)
     return jnp.sum(jnp.where(lane == own, row, 0.0), axis=1, keepdims=True)
 
 
@@ -32,7 +35,7 @@
     return jnp.sum(jnp.where(lane == own, column, 0.0), axis=0, keepdims=True)
 
 
-def correlate_kernel(place, lib_hbm, resp_hbm, coef_hbm, out, lib, resp, coef, acc, squares, sems, *, blocks, chunks):
+def correlate_kernel(place, lib_hbm, resp_hbm, coef_hbm, out, lib, resp, coef, acc, squares, sems, *, blocks, n_x, n_z):
     count = len(blocks)
     starts = [sum(blocks[:i]) for i in range(count)]
     unit = blocks[0]
@@ -84,14 +87,26 @@
             correlation(i - 1)
     correlation(count - 1)
 
-    rows = acc.shape[0] // chunks
-    tall = 2 * rows + 1
     column_sq = jnp.sum(squares[...], axis=0, keepdims=True)
-    for c in range(chunks):
-        out[c * tall:c * tall + rows, :] = acc[c * rows:(c + 1) * rows, :LANES]
-        out[c * tall + rows:c * tall + 2 * rows, :] = acc[c * rows:(c + 1) * rows, LANES:]
-        at = c * rows // LANES * LANES
-        out[c * tall + 2 * rows:(c + 1) * tall, :] = column_sq[:, at:at + LANES]
+    of_lane = lax.broadcasted_iota(jnp.int32, (1, LANES), 1)
+    run = LANES // n_z
+    tall = 4 * run + 1
+    for x in range(n_x):
+        halves = []
+        for b in range(2):
+            at = (2 * x + b) * LANES
+            corr = acc[at:at + LANES, :LANES]
+            gram = acc[at:at + LANES, LANES:].T
+            halves.append((corr, gram, column_sq[:, at:at + LANES]))
+        turned = jnp.concatenate([halves[1][2][:, LANES // 2:], halves[1][2][:, :LANES // 2]], axis=1)
+        for z in range(n_z):
+            to = (x * n_z + z) * tall
+            for part in range(2):
+                for b in range(2):
+                    out[to:to + run, :] = halves[b][part][z * run:(z + 1) * run]
+                    to += run
+            mine = (of_lane >= z * run) & (of_lane < (z + 1) * run)
+            out[to:to + 1, :] = jnp.where(mine, halves[0][2], turned)
 
 
 def block_sizes(samples):
@@ -99,13 +114,13 @@
     return (unit, 2 * unit, 3 * unit, 3 * unit, 3 * unit)
 
 
-def correlate(place, library, responses, coefficients, chunks):
+def correlate(place, library, responses, coefficients, n_x, n_z):
     samples, terms = library.shape
     blocks = block_sizes(samples)
     hbm = pl.BlockSpec(memory_space=pltpu.HBM)
     return pl.pallas_call(
-        lambda *refs: correlate_kernel(*refs, blocks=blocks, chunks=chunks),
-        out_shape=jax.ShapeDtypeStruct((2 * terms + chunks, LANES), F32),
+        lambda *refs: correlate_kernel(*refs, blocks=blocks, n_x=n_x, n_z=n_z),
+        out_shape=jax.ShapeDtypeStruct((2 * terms + n_x * n_z, LANES), F32),
         in_specs=[pl.BlockSpec(memory_space=pltpu.SMEM), hbm, hbm, hbm],
         scratch_shapes=[
             pltpu.VMEM((samples, terms), BF16),
@@ -128,16 +143,21 @@
     out[...] = total
 
 
-def first_step_kernel(place, parts, coef, send, state, *, rows, samples):
+def first_step_kernel(place, parts, coef, send, state, *, samples, n_z):
+    run = LANES // n_z
+    rows = 2 * run
     tall = 2 * rows + 1
     total = parts[0:2 * rows, :]
     column_sq = parts[2 * rows:tall, :]
-    for c in range(1, parts.shape[0] // tall):
+    for c in range(1, n_z):
         total += parts[c * tall:c * tall + 2 * rows, :]
         column_sq += parts[c * tall + 2 * rows:(c + 1) * tall, :]
-    step = STEP_SCALE * samples / to_column(column_sq, place[0] * rows % LANES, rows)
+    first = place[0] % n_z * run
+    step = STEP_SCALE * samples / to_column(column_sq, rows, first, run)
     corr, gram = total[:rows], total[rows:]
-    trial = coef[...] - step * (corr / samples)
+    at = pl.multiple_of(place[0] // n_z * 2 * LANES + first, run)
+    start = jnp.concatenate([coef[pl.ds(at, run), :], coef[pl.ds(at + LANES, run), :]], axis=0)
+    trial = start - step * (corr / samples)
     squares = to_row(jnp.sum(trial * trial, axis=1, keepdims=True))
     for c in range(8):
         send[c * (rows + 1):c * (rows + 1) + rows, :] = gram
@@ -156,39 +176,57 @@
     squares = gathered[rows:rows + 1, :]
     for c in range(1, 8):
         squares += gathered[c * (rows + 1) + rows:(c + 1) * (rows + 1), :]
-    own = shrink(state[0:rows, :], to_column(squares, 0, rows), state[2 * rows:3 * rows, :])
+    own = shrink(state[0:rows, :], to_column(squares, rows), state[2 * rows:3 * rows, :])
     own_out[...] = own
-    for c in range(32):
+    for c in range(moved.shape[0] // rows):
         moved[c * rows:(c + 1) * rows, :] = own
 
 
-def second_step_kernel(moved, coef, gathered, state, own, send, trial_out, *, rows, samples):
-    change = moved[...].astype(BF16).astype(F32) - coef[...].astype(BF16).astype(F32)
+def product_kernel(place, moved, coef, gathered, out, *, n_z):
+    run = LANES // n_z
+    rows = 2 * run
+    at = pl.multiple_of(place[0] // n_z * 2 * LANES, LANES)
+    total = jnp.zeros((LANES, LANES), F32)
+    for b in range(2):
+        new = jnp.concatenate(
+            [moved[z * rows + b * run:z * rows + (b + 1) * run, :] for z in range(n_z)], axis=0
+        )
+        old = coef[pl.ds(at + b * LANES, LANES), :]
+        change = new.astype(BF16).astype(F32) - old.astype(BF16).astype(F32)
+        gram = jnp.concatenate(
+            [gathered[r * (rows + 1) + b * run:r * (rows + 1) + (b + 1) * run, :] for r in range(8)], axis=0
+        )
+        total += jnp.dot(gram, change, precision=lax.Precision.HIGHEST, preferred_element_type=F32)
+    out[...] = total
+
+
+def second_step_kernel(products, state, own, send, trial_out, *, rows, samples):
     corr = state[rows:2 * rows, :]
-    for c in range(8):
-        corr += jnp.dot(
-            gathered[c * (rows + 1):c * (rows + 1) + rows, :],
-            change[c * LANES:(c + 1) * LANES, :],
-            precision=lax.Precision.HIGHEST,
-            preferred_element_type=F32,
-        )
+    for c in range(products.shape[0] // rows):
+        corr += products[c * rows:(c + 1) * rows, :]
     trial = own[...] - state[2 * rows:3 * rows, :] * (corr / samples)
     squares = to_row(jnp.sum(trial * trial, axis=1, keepdims=True))
-    send[...] = jnp.broadcast_to(squares, (8, LANES))
+    send[...] = jnp.broadcast_to(squares, send.shape)
     trial_out[...] = trial
 
 
 def second_shrink_kernel(squares, trial, state, moved, *, rows):
     total = jnp.sum(squares[...], axis=0, keepdims=True)
-    own = shrink(trial[...], to_column(total, 0, rows), state[2 * rows:3 * rows, :])
-    for c in range(32):
+    own = shrink(trial[...], to_column(total, rows), state[2 * rows:3 * rows, :])
+    for c in range(moved.shape[0] // rows):
         moved[c * rows:(c + 1) * rows, :] = own
 
 
-def whole(kernel, name, out_shapes, *arrays, **fixed):
+def whole(kernel, name, out_shapes, *arrays, place=None, **fixed):
+    vmem = pl.BlockSpec(memory_space=pltpu.VMEM)
+    in_specs = [vmem] * len(arrays)
+    if place is not None:
+        arrays, in_specs = (place, *arrays), [pl.BlockSpec(memory_space=pltpu.SMEM), *in_specs]
     return pl.pallas_call(
         lambda *refs: kernel(*refs, **fixed),
         out_shape=[jax.ShapeDtypeStruct(s, F32) for s in out_shapes],
+        in_specs=in_specs,
+        out_specs=[vmem] * len(out_shapes),
         compiler_params=params(),
         name=name,
     )(*arrays)
@@ -204,52 +242,40 @@
     samples, terms = library.shape[0] * n_samp, library.shape[1]
     rows = terms // n_samp
     place = jnp.stack([lax.axis_index("samp"), lax.axis_index("reg")]).astype(jnp.int32)
-
     n_z = n_samp // N_X
     over_x = [[x * n_z + z for x in range(N_X)] for z in range(n_z)]
     over_z = [[x * n_z + z for z in range(n_z)] for x in range(N_X)]
-    parts = correlate(place, library, responses, coefficients, n_samp)
+
+    parts = correlate(place, library, responses, coefficients, N_X, n_z)
     parts = exchange(parts, "samp", N_X, over_x)
     (parts,) = whole(add_kernel, "add", [(parts.shape[0] // N_X, LANES)], parts)
     parts = exchange(parts, "samp", n_z, over_z)
 
-    send, state = pl.pallas_call(
-        lambda *refs: first_step_kernel(*refs, rows=rows, samples=samples),
-        out_shape=[
-            jax.ShapeDtypeStruct((n_reg * (rows + 1), LANES), F32),
-            jax.ShapeDtypeStruct((3 * rows, LANES), F32),
-        ],
-        grid_spec=pltpu.PrefetchScalarGridSpec(
-            num_scalar_prefetch=1,
-            grid=(1,),
-            in_specs=[
-                pl.BlockSpec(parts.shape, lambda i, place: (0, 0)),
-                pl.BlockSpec((rows, LANES), lambda i, place: (place[0], 0)),
-            ],
-            out_specs=[
-                pl.BlockSpec((n_reg * (rows + 1), LANES), lambda i, place: (0, 0)),
-                pl.BlockSpec((3 * rows, LANES), lambda i, place: (0, 0)),
-            ],
-        ),
-        compiler_params=params(),
-        name="first_step",
-    )(place, parts, coefficients)
+    send, state = whole(
+        first_step_kernel, "first_step", [(n_reg * (rows + 1), LANES), (3 * rows, LANES)],
+        parts, coefficients, place=place, samples=samples, n_z=n_z,
+    )
     gathered = exchange(send, "reg", n_reg)
-
     spread, own = whole(
-        first_shrink_kernel, "first_shrink", [(terms, LANES), (rows, LANES)], gathered, state, rows=rows
-    )
-    moved = exchange(spread, "samp", n_samp)
-
+        first_shrink_kernel, "first_shrink", [(n_z * rows, LANES), (rows, LANES)], gathered, state, rows=rows
+    )
+    moved = exchange(spread, "samp", n_z, over_z)
+
+    (products,) = whole(
+        product_kernel, "product", [(LANES, LANES)], moved, coefficients, gathered, place=place, n_z=n_z
+    )
+    products = exchange(products, "samp", N_X, over_x)
     send, trial = whole(
         second_step_kernel, "second_step", [(n_reg, LANES), (rows, LANES)],
-        moved, coefficients, gathered, state, own, rows=rows, samples=samples,
+        products, state, own, rows=rows, samples=samples,
     )
     squares = exchange(send, "reg", n_reg)
     (spread,) = whole(
         second_shrink_kernel, "second_shrink", [(terms, LANES)], squares, trial, state, rows=rows
     )
-    return exchange(spread, "samp", n_samp)
+    moved = exchange(spread, "samp", n_samp)
+    moved = moved.reshape(N_X, n_z, 2, rows // 2, LANES).transpose(0, 2, 1, 3, 4)
+    return moved.reshape(terms, LANES)
 
 
 def solution(mesh):

time: 109 us -> 107 us (0.982)
  blocking collectives: 99.5 us -> 96.9 us
    all_to_all x6 -> x7, blocking collectives: 99.5 us -> 96.9 us  [exchange(): lax.all_to_all(blocks, axis, 0, 0, axis_index_groups=groups)]
    pallas_call x2 -> x1, Pallas kernels: 7.61 us -> 6.96 us  [correlate(): pl.pallas_call(lambda *refs: correlate_kernel(*refs, blocks=blocks, n_x=n...]
where the time goes in v5:
time: 107 us
  blocking collectives  96.9 us (91%)
  Pallas kernels  8.91 us (8%)
    all_to_all x7, blocking collectives, exchange(): lax.all_to_all(blocks, axis, 0, 0, axis_index_groups=groups)  96.9 us
    pallas_call x1, Pallas kernels, correlate(): pl.pallas_call(lambda *refs: correlate_kernel(*refs, blocks=blocks, n_x=n...  6.96 us

profile of v5, /device:TPU:32, one launch (start us, length us, event | category | flops | bytes accessed | tf_op | source)
XLA Modules:
  0.0 106.8 jit_solution(5389009634567266045)
XLA Ops:
  0.0 0.1 pad_add_fusion.refs_0_
  0.1 7.0 %correlate.1 = f32[2080,128]{1,0:T(8,128)S(1)} custom-call(s32[2]{0:T(128)S(1)} %pad_add_fusion.refs_0_, bf16[3072,1024]{1,0:T(8,128)(2,1)} %refs_1_.1, bf16[3072,128]{1,0:T(8,128)(2,1)} %refs_2_.3, f32[1024,128]{1,0:T(8,128)} %refs_2_.5), custom_call_target="tpu_custom_call" | custom-call | tf_op jit(solution)/shard_map/correlate/pallas_call | solution.py:121
  7.0 19.4 %all_to_all.35 = f32[4,520,1,128]{3,1,2,0:T(8,128)S(1)} all-to-all(f32[4,520,1,128]{3,1,2,0:T(8,128)S(1)} %bitcast.29), channel_id=1, replica_groups={{0,64,128,192},{8,72,136,200},{16,80,144,208},{24,88,152,216},{32,96,16..., dimensions={0} | all-to-all | bytes 2129920 | tf_op jit(solution)/shard_map/all_to_all | solution.py:237
  26.4 0.0 copy-start
  26.5 17.8 %all_to_all.36 = f32[8,65,1,128]{3,2,1,0:T(1,128)S(1)} all-to-all(f32[8,65,1,128]{3,2,1,0:T(1,128)S(1)} %bitcast.35), channel_id=1, replica_groups={{0,8,16,24,32,40,48,56},{64,72,80,88,96,104,112,120},{128,136,144,152,1..., dimensions={0} | all-to-all | bytes 532480 | tf_op jit(solution)/shard_map/all_to_all | solution.py:237
  44.3 0.0 copy-done
  44.3 0.7 first_step.1
  45.0 10.5 %all_to_all.37 = f32[8,33,1,128]{3,2,1,0:T(1,128)S(1)} all-to-all(f32[8,33,1,128]{3,2,1,0:T(1,128)S(1)} %bitcast.39), channel_id=1, replica_groups=mesh['samp'=32,'reg'=8] {'reg'}, dimensions={0} | all-to-all | bytes 270336 | tf_op jit(solution)/shard_map/all_to_all | solution.py:237
  55.5 0.1 first_shrink.1
  55.6 11.5 %all_to_all.38 = f32[8,32,1,128]{3,1,2,0:T(8,128)S(1)} all-to-all(f32[8,32,1,128]{3,1,2,0:T(8,128)S(1)} %bitcast.40), channel_id=1, replica_groups={{0,8,16,24,32,40,48,56},{64,72,80,88,96,104,112,120},{128,136,144,152,1..., dimensions={0} | all-to-all | bytes 262144 | tf_op jit(solution)/shard_map/all_to_all | solution.py:237
  67.1 0.8 product.1
  68.0 8.0 %all_to_all.39 = f32[4,32,1,128]{3,1,2,0:T(8,128)S(1)} all-to-all(f32[4,32,1,128]{3,1,2,0:T(8,128)S(1)} %bitcast.37), channel_id=1, replica_groups={{0,64,128,192},{8,72,136,200},{16,80,144,208},{24,88,152,216},{32,96,16..., dimensions={0} | all-to-all | bytes 131072 | tf_op jit(solution)/shard_map/all_to_all | solution.py:237
  76.0 0.1 second_step.1
  76.1 7.6 %all_to_all.40 = f32[8,1,1,128]{3,2,1,0:T(1,128)S(1)} all-to-all(f32[8,1,1,128]{3,2,1,0:T(1,128)S(1)} %bitcast.42), channel_id=1, replica_groups=mesh['samp'=32,'reg'=8] {'reg'}, dimensions={0} | all-to-all | bytes 8192 | tf_op jit(solution)/shard_map/all_to_all | solution.py:237
  83.7 0.1 second_shrink.1
  83.8 22.1 %all_to_all.41 = f32[32,32,1,128]{3,1,2,0:T(8,128)S(1)} all-to-all(f32[32,32,1,128]{3,1,2,0:T(8,128)S(1)} %bitcast.31), channel_id=1, replica_groups=mesh['samp'=32,'reg'=8] {'samp'}, dimensions={0} | all-to-all | bytes 1048576 | tf_op jit(solution)/shard_map/all_to_all | solution.py:237
  105.9 0.8 copy.13
  (1 shorter events, 0.0 us)
Async XLA Ops:
  26.4 17.9 %copy-start = (f32[1024,128]{1,0:T(8,128)S(1)}, f32[1024,128]{1,0:T(8,128)}, u32[]{:S(2)}) copy-start(f32[1024,128]{1,0:T(8,128)} %refs_2_.5) | copy-start | bytes 1572868

commit v6 on v5

--- a/solution.py
+++ b/solution.py
@@ -35,7 +35,7 @@
     return jnp.sum(jnp.where(lane == own, column, 0.0), axis=0, keepdims=True)
 
 
-def correlate_kernel(place, lib_hbm, resp_hbm, coef_hbm, out, lib, resp, coef, acc, squares, sems, *, blocks, n_x, n_z):
+def correlate_kernel(lib_hbm, resp_hbm, coef_hbm, out, lib, resp, coef, acc, squares, sems, *, blocks, n_x, n_z):
     count = len(blocks)
     starts = [sum(blocks[:i]) for i in range(count)]
     unit = blocks[0]
@@ -57,7 +57,7 @@
             copy.start()
     copy_coef.wait()
     weights = coef[...].astype(BF16)
-    columns = pl.multiple_of(place[1] * LANES, LANES)
+    columns = pl.multiple_of(lax.axis_index("reg") * LANES, LANES)
     residuals = {}
 
     def residual(i):
@@ -114,14 +114,14 @@
     return (unit, 2 * unit, 3 * unit, 3 * unit, 3 * unit)
 
 
-def correlate(place, library, responses, coefficients, n_x, n_z):
+def correlate(library, responses, coefficients, n_x, n_z):
     samples, terms = library.shape
     blocks = block_sizes(samples)
     hbm = pl.BlockSpec(memory_space=pltpu.HBM)
     return pl.pallas_call(
         lambda *refs: correlate_kernel(*refs, blocks=blocks, n_x=n_x, n_z=n_z),
         out_shape=jax.ShapeDtypeStruct((2 * terms + n_x * n_z, LANES), F32),
-        in_specs=[pl.BlockSpec(memory_space=pltpu.SMEM), hbm, hbm, hbm],
+        in_specs=[hbm, hbm, hbm],
         scratch_shapes=[
             pltpu.VMEM((samples, terms), BF16),
             pltpu.VMEM((samples, LANES), BF16),
@@ -132,7 +132,7 @@
         ],
         compiler_params=params(),
         name="correlate",
-    )(place, library, *(pltpu.with_memory_space_constraint(a, pltpu.HBM) for a in (responses, coefficients)))
+    )(library, *(pltpu.with_memory_space_constraint(a, pltpu.HBM) for a in (responses, coefficients)))
 
 
 def add_kernel(parts, out):
@@ -143,7 +143,7 @@
     out[...] = total
 
 
-def first_step_kernel(place, parts, coef, send, state, *, samples, n_z):
+def first_step_kernel(parts, coef, send, state, *, samples, n_z):
     run = LANES // n_z
     rows = 2 * run
     tall = 2 * rows + 1
@@ -152,10 +152,11 @@
     for c in range(1, n_z):
         total += parts[c * tall:c * tall + 2 * rows, :]
         column_sq += parts[c * tall + 2 * rows:(c + 1) * tall, :]
-    first = place[0] % n_z * run
+    samp = lax.axis_index("samp")
+    first = samp % n_z * run
     step = STEP_SCALE * samples / to_column(column_sq, rows, first, run)
     corr, gram = total[:rows], total[rows:]
-    at = pl.multiple_of(place[0] // n_z * 2 * LANES + first, run)
+    at = pl.multiple_of(samp // n_z * 2 * LANES + first, run)
     start = jnp.concatenate([coef[pl.ds(at, run), :], coef[pl.ds(at + LANES, run), :]], axis=0)
     trial = start - step * (corr / samples)
     squares = to_row(jnp.sum(trial * trial, axis=1, keepdims=True))
@@ -182,22 +183,26 @@
         moved[c * rows:(c + 1) * rows, :] = own
 
 
-def product_kernel(place, moved, coef, gathered, out, *, n_z):
+def product_kernel(moved, coef, gathered, out, *, n_z):
     run = LANES // n_z
     rows = 2 * run
-    at = pl.multiple_of(place[0] // n_z * 2 * LANES, LANES)
-    total = jnp.zeros((LANES, LANES), F32)
+    at = pl.multiple_of(lax.axis_index("samp") // n_z * 2 * LANES, 2 * LANES)
+    new, gram = [], []
     for b in range(2):
-        new = jnp.concatenate(
-            [moved[z * rows + b * run:z * rows + (b + 1) * run, :] for z in range(n_z)], axis=0
-        )
-        old = coef[pl.ds(at + b * LANES, LANES), :]
-        change = new.astype(BF16).astype(F32) - old.astype(BF16).astype(F32)
-        gram = jnp.concatenate(
+        new += [moved[z * rows + b * run:z * rows + (b + 1) * run, :] for z in range(n_z)]
+        gram.append(jnp.concatenate(
             [gathered[r * (rows + 1) + b * run:r * (rows + 1) + (b + 1) * run, :] for r in range(8)], axis=0
-        )
-        total += jnp.dot(gram, change, precision=lax.Precision.HIGHEST, preferred_element_type=F32)
-    out[...] = total
+        ))
+    new = jnp.concatenate(new, axis=0).astype(BF16)
+    old = coef[pl.ds(at, 2 * LANES), :].astype(BF16)
+    both = jnp.concatenate([new, old], axis=1)
+    rest = jnp.concatenate(gram, axis=1)
+    total = jnp.zeros((LANES, 2 * LANES), F32)
+    for _ in range(3):
+        part = rest.astype(BF16)
+        rest = rest - part.astype(F32)
+        total += jnp.dot(part, both, preferred_element_type=F32)
+    out[...] = total[:, :LANES] - total[:, LANES:]
 
 
 def second_step_kernel(products, state, own, send, trial_out, *, rows, samples):
@@ -217,15 +222,12 @@
         moved[c * rows:(c + 1) * rows, :] = own
 
 
-def whole(kernel, name, out_shapes, *arrays, place=None, **fixed):
+def whole(kernel, name, out_shapes, *arrays, **fixed):
     vmem = pl.BlockSpec(memory_space=pltpu.VMEM)
-    in_specs = [vmem] * len(arrays)
-    if place is not None:
-        arrays, in_specs = (place, *arrays), [pl.BlockSpec(memory_space=pltpu.SMEM), *in_specs]
     return pl.pallas_call(
         lambda *refs: kernel(*refs, **fixed),
         out_shape=[jax.ShapeDtypeStruct(s, F32) for s in out_shapes],
-        in_specs=in_specs,
+        in_specs=[vmem] * len(arrays),
         out_specs=[vmem] * len(out_shapes),
         compiler_params=params(),
         name=name,
@@ -241,19 +243,18 @@
     n_samp, n_reg = lax.axis_size("samp"), lax.axis_size("reg")
     samples, terms = library.shape[0] * n_samp, library.shape[1]
     rows = terms // n_samp
-    place = jnp.stack([lax.axis_index("samp"), lax.axis_index("reg")]).astype(jnp.int32)
     n_z = n_samp // N_X
     over_x = [[x * n_z + z for x in range(N_X)] for z in range(n_z)]
     over_z = [[x * n_z + z for z in range(n_z)] for x in range(N_X)]
 
-    parts = correlate(place, library, responses, coefficients, N_X, n_z)
+    parts = correlate(library, responses, coefficients, N_X, n_z)
     parts = exchange(parts, "samp", N_X, over_x)
     (parts,) = whole(add_kernel, "add", [(parts.shape[0] // N_X, LANES)], parts)
     parts = exchange(parts, "samp", n_z, over_z)
 
     send, state = whole(
         first_step_kernel, "first_step", [(n_reg * (rows + 1), LANES), (3 * rows, LANES)],
-        parts, coefficients, place=place, samples=samples, n_z=n_z,
+        parts, coefficients, samples=samples, n_z=n_z,
     )
     gathered = exchange(send, "reg", n_reg)
     spread, own = whole(
@@ -262,7 +263,7 @@
     moved = exchange(spread, "samp", n_z, over_z)
 
     (products,) = whole(
-        product_kernel, "product", [(LANES, LANES)], moved, coefficients, gathered, place=place, n_z=n_z
+        product_kernel, "product", [(LANES, LANES)], moved, coefficients, gathered, n_z=n_z
     )
     products = exchange(products, "samp", N_X, over_x)
     send, trial = whole(

time: 107 us -> 105 us (0.981)
  Pallas kernels: 8.91 us -> 7.24 us
    pallas_call x6, Pallas kernels: 1.95 us -> 0.82 us  [whole(): pl.pallas_call(lambda *refs: kernel(*refs, **fixed), out_shape=[jax.Shape...]
where the time goes in v6:
time: 105 us
  blocking collectives  96.9 us (92%)
  Pallas kernels  7.24 us (7%)
    all_to_all x7, blocking collectives, exchange(): lax.all_to_all(blocks, axis, 0, 0, axis_index_groups=groups)  96.9 us
    pallas_call x1, Pallas kernels, correlate(): pl.pallas_call(lambda *refs: correlate_kernel(*refs, blocks=blocks, n_x=n...  6.42 us

profile of v6, /device:TPU:32, one launch (start us, length us, event | category | flops | bytes accessed | tf_op | source)
XLA Modules:
  0.0 105.0 jit_solution(8920902871620138304)
XLA Ops:
  0.0 6.4 %correlate.1 = f32[2080,128]{1,0:T(8,128)S(1)} custom-call(bf16[3072,1024]{1,0:T(8,128)(2,1)} %refs_0_.1, bf16[3072,128]{1,0:T(8,128)(2,1)} %refs_1_.3, f32[1024,128]{1,0:T(8,128)} %refs_1_.5), custom_call_target="tpu_custom_call" | custom-call | tf_op jit(solution)/shard_map/correlate/pallas_call | solution.py:121
  6.4 19.4 %all_to_all.35 = f32[4,520,1,128]{3,1,2,0:T(8,128)S(1)} all-to-all(f32[4,520,1,128]{3,1,2,0:T(8,128)S(1)} %bitcast.27), channel_id=1, replica_groups={{0,64,128,192},{8,72,136,200},{16,80,144,208},{24,88,152,216},{32,96,16..., dimensions={0} | all-to-all | bytes 2129920 | tf_op jit(solution)/shard_map/all_to_all | solution.py:239
  25.8 0.0 copy-start
  25.8 17.8 %all_to_all.36 = f32[8,65,1,128]{3,2,1,0:T(1,128)S(1)} all-to-all(f32[8,65,1,128]{3,2,1,0:T(1,128)S(1)} %bitcast.33), channel_id=1, replica_groups={{0,8,16,24,32,40,48,56},{64,72,80,88,96,104,112,120},{128,136,144,152,1..., dimensions={0} | all-to-all | bytes 532480 | tf_op jit(solution)/shard_map/all_to_all | solution.py:239
  43.7 0.0 copy-done
  43.7 0.2 first_step.1
  43.9 10.5 %all_to_all.37 = f32[8,33,1,128]{3,2,1,0:T(1,128)S(1)} all-to-all(f32[8,33,1,128]{3,2,1,0:T(1,128)S(1)} %bitcast.37), channel_id=1, replica_groups=mesh['samp'=32,'reg'=8] {'reg'}, dimensions={0} | all-to-all | bytes 270336 | tf_op jit(solution)/shard_map/all_to_all | solution.py:239
  54.3 0.1 first_shrink.1
  54.4 11.5 %all_to_all.38 = f32[8,32,1,128]{3,1,2,0:T(8,128)S(1)} all-to-all(f32[8,32,1,128]{3,1,2,0:T(8,128)S(1)} %bitcast.38), channel_id=1, replica_groups={{0,8,16,24,32,40,48,56},{64,72,80,88,96,104,112,120},{128,136,144,152,1..., dimensions={0} | all-to-all | bytes 262144 | tf_op jit(solution)/shard_map/all_to_all | solution.py:239
  66.0 0.2 product.1
  66.2 8.0 %all_to_all.39 = f32[4,32,1,128]{3,1,2,0:T(8,128)S(1)} all-to-all(f32[4,32,1,128]{3,1,2,0:T(8,128)S(1)} %bitcast.36), channel_id=1, replica_groups={{0,64,128,192},{8,72,136,200},{16,80,144,208},{24,88,152,216},{32,96,16..., dimensions={0} | all-to-all | bytes 131072 | tf_op jit(solution)/shard_map/all_to_all | solution.py:239
  74.2 0.1 second_step.1
  74.3 7.6 %all_to_all.40 = f32[8,1,1,128]{3,2,1,0:T(1,128)S(1)} all-to-all(f32[8,1,1,128]{3,2,1,0:T(1,128)S(1)} %bitcast.40), channel_id=1, replica_groups=mesh['samp'=32,'reg'=8] {'reg'}, dimensions={0} | all-to-all | bytes 8192 | tf_op jit(solution)/shard_map/all_to_all | solution.py:239
  81.9 0.1 second_shrink.1
  82.1 22.1 %all_to_all.41 = f32[32,32,1,128]{3,1,2,0:T(8,128)S(1)} all-to-all(f32[32,32,1,128]{3,1,2,0:T(8,128)S(1)} %bitcast.29), channel_id=1, replica_groups=mesh['samp'=32,'reg'=8] {'samp'}, dimensions={0} | all-to-all | bytes 1048576 | tf_op jit(solution)/shard_map/all_to_all | solution.py:239
  104.2 0.8 copy.13
  (1 shorter events, 0.0 us)
Async XLA Ops:
  25.8 17.9 %copy-start = (f32[1024,128]{1,0:T(8,128)S(1)}, f32[1024,128]{1,0:T(8,128)}, u32[]{:S(2)}) copy-start(f32[1024,128]{1,0:T(8,128)} %refs_1_.5) | copy-start | bytes 1572868

commit v7 on v6

--- a/solution.py
+++ b/solution.py
@@ -71,7 +71,7 @@
         at = pl.ds(starts[i], blocks[i])
         block = lib[at, :]
         right = jnp.concatenate([residuals[i], lib[at, pl.ds(columns, LANES)]], axis=1)
-        part = lax.dot_general(block, right, (((0,), (0,)), ((), ())), preferred_element_type=F32)
+        part = lax.dot_general(right, block, (((0,), (0,)), ((), ())), preferred_element_type=F32)
         wide = block.astype(F32)
         part_sq = jnp.sum((wide * wide).reshape(-1, 8, wide.shape[1]), axis=0)
         if i == 0:
@@ -95,8 +95,8 @@
         halves = []
         for b in range(2):
             at = (2 * x + b) * LANES
-            corr = acc[at:at + LANES, :LANES]
-            gram = acc[at:at + LANES, LANES:].T
+            corr = acc[:LANES, at:at + LANES].T
+            gram = acc[LANES:, at:at + LANES]
             halves.append((corr, gram, column_sq[:, at:at + LANES]))
         turned = jnp.concatenate([halves[1][2][:, LANES // 2:], halves[1][2][:, :LANES // 2]], axis=1)
         for z in range(n_z):
@@ -126,7 +126,7 @@
             pltpu.VMEM((samples, terms), BF16),
             pltpu.VMEM((samples, LANES), BF16),
             pltpu.VMEM((terms, LANES), F32),
-            pltpu.VMEM((terms, 2 * LANES), F32),
+            pltpu.VMEM((2 * LANES, terms), F32),
             pltpu.VMEM((8, terms), F32),
             pltpu.SemaphoreType.DMA((1 + samples // blocks[0] + len(blocks),)),
         ],

time: 105 us -> 105 us (level)
  no operation moved by 1% of the time
where the time goes in v7:
time: 105 us
  blocking collectives  96.9 us (92%)
  Pallas kernels  7.15 us (7%)
    all_to_all x7, blocking collectives, exchange(): lax.all_to_all(blocks, axis, 0, 0, axis_index_groups=groups)  96.9 us
    pallas_call x1, Pallas kernels, correlate(): pl.pallas_call(lambda *refs: correlate_kernel(*refs, blocks=blocks, n_x=n...  6.33 us

profile of v7, /device:TPU:32, one launch (start us, length us, event | category | flops | bytes accessed | tf_op | source)
XLA Modules:
  0.0 104.9 jit_solution(14025901316460197040)
XLA Ops:
  0.0 6.3 %correlate.1 = f32[2080,128]{1,0:T(8,128)S(1)} custom-call(bf16[3072,1024]{1,0:T(8,128)(2,1)} %refs_0_.1, bf16[3072,128]{1,0:T(8,128)(2,1)} %refs_1_.3, f32[1024,128]{1,0:T(8,128)} %refs_1_.5), custom_call_target="tpu_custom_call" | custom-call | tf_op jit(solution)/shard_map/correlate/pallas_call | solution.py:121
  6.3 19.4 %all_to_all.35 = f32[4,520,1,128]{3,1,2,0:T(8,128)S(1)} all-to-all(f32[4,520,1,128]{3,1,2,0:T(8,128)S(1)} %bitcast.27), channel_id=1, replica_groups={{0,64,128,192},{8,72,136,200},{16,80,144,208},{24,88,152,216},{32,96,16..., dimensions={0} | all-to-all | bytes 2129920 | tf_op jit(solution)/shard_map/all_to_all | solution.py:239
  25.7 0.0 copy-start
  25.8 17.8 %all_to_all.36 = f32[8,65,1,128]{3,2,1,0:T(1,128)S(1)} all-to-all(f32[8,65,1,128]{3,2,1,0:T(1,128)S(1)} %bitcast.33), channel_id=1, replica_groups={{0,8,16,24,32,40,48,56},{64,72,80,88,96,104,112,120},{128,136,144,152,1..., dimensions={0} | all-to-all | bytes 532480 | tf_op jit(solution)/shard_map/all_to_all | solution.py:239
  43.6 0.0 copy-done
  43.6 0.2 first_step.1
  43.8 10.5 %all_to_all.37 = f32[8,33,1,128]{3,2,1,0:T(1,128)S(1)} all-to-all(f32[8,33,1,128]{3,2,1,0:T(1,128)S(1)} %bitcast.37), channel_id=1, replica_groups=mesh['samp'=32,'reg'=8] {'reg'}, dimensions={0} | all-to-all | bytes 270336 | tf_op jit(solution)/shard_map/all_to_all | solution.py:239
  54.2 0.1 first_shrink.1
  54.3 11.5 %all_to_all.38 = f32[8,32,1,128]{3,1,2,0:T(8,128)S(1)} all-to-all(f32[8,32,1,128]{3,1,2,0:T(8,128)S(1)} %bitcast.38), channel_id=1, replica_groups={{0,8,16,24,32,40,48,56},{64,72,80,88,96,104,112,120},{128,136,144,152,1..., dimensions={0} | all-to-all | bytes 262144 | tf_op jit(solution)/shard_map/all_to_all | solution.py:239
  65.9 0.2 product.1
  66.1 8.0 %all_to_all.39 = f32[4,32,1,128]{3,1,2,0:T(8,128)S(1)} all-to-all(f32[4,32,1,128]{3,1,2,0:T(8,128)S(1)} %bitcast.36), channel_id=1, replica_groups={{0,64,128,192},{8,72,136,200},{16,80,144,208},{24,88,152,216},{32,96,16..., dimensions={0} | all-to-all | bytes 131072 | tf_op jit(solution)/shard_map/all_to_all | solution.py:239
  74.1 0.1 second_step.1
  74.2 7.6 %all_to_all.40 = f32[8,1,1,128]{3,2,1,0:T(1,128)S(1)} all-to-all(f32[8,1,1,128]{3,2,1,0:T(1,128)S(1)} %bitcast.40), channel_id=1, replica_groups=mesh['samp'=32,'reg'=8] {'reg'}, dimensions={0} | all-to-all | bytes 8192 | tf_op jit(solution)/shard_map/all_to_all | solution.py:239
  81.8 0.1 second_shrink.1
  82.0 22.1 %all_to_all.41 = f32[32,32,1,128]{3,1,2,0:T(8,128)S(1)} all-to-all(f32[32,32,1,128]{3,1,2,0:T(8,128)S(1)} %bitcast.29), channel_id=1, replica_groups=mesh['samp'=32,'reg'=8] {'samp'}, dimensions={0} | all-to-all | bytes 1048576 | tf_op jit(solution)/shard_map/all_to_all | solution.py:239
  104.1 0.8 copy.13
  (1 shorter events, 0.0 us)
Async XLA Ops:
  25.7 17.9 %copy-start = (f32[1024,128]{1,0:T(8,128)S(1)}, f32[1024,128]{1,0:T(8,128)}, u32[]{:S(2)}) copy-start(f32[1024,128]{1,0:T(8,128)} %refs_1_.5) | copy-start | bytes 1572868
